TPU v7x, 256 devices: a whole 4x4x8 slice. The times are simulated.
256 devices in a mesh: ctx: 32 (over z, x), grp: 8 (over y, core).
Axes of the slice: x: 4, y: 4, z: 8, core: 2. Of those that a mesh axis runs over, the one named last changes fastest.
Arguments:
- query: bfloat16 [512, 5120], P('ctx', 'grp'), may hold values from -8 to 8
- keys: bfloat16 [131072, 1024], P('ctx', 'grp'), may hold values from -16 to 16
- values: bfloat16 [131072, 1024], P('ctx', 'grp'), may hold values from -6 to 6
- blocks: int32 [512, 32, 8], P(None, 'ctx'), may hold values from 0 to 31, as said below
Outputs:
- attended: bfloat16 [512, 5120], P(('ctx', 'grp'))
Inputs may be any that keep to these rules, and one draw needn't show every extreme that they name: Each row's list for each context shard names 8 different blocks, the first of them block 0.
All inputs are finite; a program needn't handle non-finite values.
Results may differ from a plain program's by a relative error of at most 0.012.
Values may be sent and summed in bfloat16 or wider, within the bound.
No kernel may reach another device: no remote copies, remote signals or barrier semaphores. Data moves between devices by JAX's collectives and lax.ppermute only.
A program may use at most 192 MiB of HBM per device.

v0:
```python
import math

import jax
import jax.numpy as jnp
from jax import lax
from jax.sharding import PartitionSpec as P

HD = 128
QPK = 5
BLOCK = 128


def per_device(query, keys, values, blocks):
    whole = lax.all_gather(query, "ctx", axis=0, tiled=True)
    row_count = whole.shape[0]
    ctx_dev = keys.shape[0]
    score_scale = 1.0 / math.sqrt(HD)
    listed_here = blocks[:, 0, :]
    block_count = ctx_dev // BLOCK
    block_ids = jnp.arange(block_count, dtype=jnp.int32)
    listed_hits = jnp.any(listed_here[:, :, None] == block_ids[None, None, :], axis=1)
    key_span = min(512, ctx_dev)
    turn_count = ctx_dev // key_span
    span_blocks = key_span // BLOCK
    query_group = whole.reshape(row_count * QPK, HD)

    def scores_at(block_index):
        key_block = lax.dynamic_slice_in_dim(keys, block_index * key_span, key_span, 0)
        scores = jnp.einsum("id,td->it", query_group, key_block, preferred_element_type=jnp.float32)
        scores = scores.reshape(row_count, QPK, key_span) * score_scale
        block_hits = lax.dynamic_slice_in_dim(
            listed_hits, block_index * span_blocks, span_blocks, 1
        )
        block_mask = jnp.repeat(block_hits, BLOCK, axis=1)[:, None, :]
        return (scores, block_mask)

    def first_pass(block_index, running_max):
        scores, block_mask = scores_at(block_index)
        return jnp.maximum(running_max, jnp.max(jnp.where(block_mask, scores, -jnp.inf), axis=-1))

    local_max = lax.fori_loop(
        0, turn_count, first_pass, jnp.full((row_count, QPK), -jnp.inf, jnp.float32)
    )

    def second_pass(block_index, carry):
        denominator, numerator = carry
        scores, block_mask = scores_at(block_index)
        weights = jnp.where(block_mask, jnp.exp(scores - local_max[..., None]), 0.0)
        denominator = denominator + jnp.sum(weights, axis=-1)
        rounded = weights.astype(jnp.bfloat16).reshape(row_count * QPK, key_span)
        value_block = lax.dynamic_slice_in_dim(values, block_index * key_span, key_span, 0)
        numerator = numerator + jnp.dot(rounded, value_block, preferred_element_type=jnp.float32)
        return (denominator, numerator)

    start_carry = (
        jnp.zeros((row_count, QPK), jnp.float32),
        jnp.zeros((row_count * QPK, HD), jnp.float32),
    )
    local_sum, local_out = lax.fori_loop(0, turn_count, second_pass, start_carry)
    out_parts = local_out.reshape(row_count, QPK * HD)
    part_out = (out_parts / jnp.repeat(local_sum, HD, axis=1)).astype(jnp.bfloat16)
    log_total = local_max + jnp.log(local_sum)
    global_top = lax.pmax(log_total, "ctx")
    factor = jnp.exp(log_total - global_top)
    scaled_out = part_out.astype(jnp.float32) * jnp.repeat(factor, HD, axis=1)
    numerator, denominator = (
        lax.psum_scatter(scaled_out, "ctx", scatter_dimension=0, tiled=True),
        lax.psum_scatter(factor, "ctx", scatter_dimension=0, tiled=True),
    )
    finished = (numerator / jnp.repeat(denominator, HD, axis=1)).astype(jnp.bfloat16)
    return lax.all_to_all(finished, "grp", split_axis=0, concat_axis=1, tiled=True)


def solution(mesh):
    placed = (P("ctx", "grp"), P("ctx", "grp"), P("ctx", "grp"), P(None, "ctx", None))
    return jax.shard_map(
        per_device, mesh=mesh, in_specs=placed, out_specs=P(("ctx", "grp"), None), check_vma=False
    )
```

profile of v0, /device:TPU:1, one launch (start us, length us, event | category | flops | bytes accessed | tf_op | source)
XLA Modules:
  0.0 819.6 jit_solution(16259383982873742512)
XLA Ops:
  7.5 42.3 %all_gather.3 = bf16[512,640]{1,0:T(8,128)(2,1)S(1)} all-gather(bf16[16,640]{1,0:T(8,128)(2,1)} %param.8), channel_id=1, replica_groups=mesh['ctx'=32,'grp'=8] {'ctx'}, dimensions={0}, use_global_device_ids=true | all-gather | bytes 675840 | tf_op jit(solution)/shard_map/all_gather | solution.py:14
  51.1 68.9 %while.31 = (s32[]{:T(128)}, f32[512,5]{1,0:T(8,128)}, pred[512,32]{1,0:T(8,128)(4,1)S(1)}, bf16[4096,128]{1,0:T(8,128)(2,1)}, bf16[2560,128]{1,0:T(8,128)(2,1)}...) while((s32[]{:T(128)}, f32[512,5]{1,0:T(8,128)}, ...), condition=%wide.region_3.4_spmd.clone, body=%wide.region_1.3_spmd.clone.sunk | while | flops 339479040 | bytes 12470583 | solution.py:41
  121.1 96.1 %while.32 = (s32[]{:T(128)}, f32[512,5]{1,0:T(8,128)}, f32[2560,128]{1,0:T(8,128)}, pred[512,32]{1,0:T(8,128)(4,1)S(1)}, bf16[4096,128]{1,0:T(8,128)(2,1)}, /*in...) while((s32[]{:T(128)}, f32[512,5]{1,0:T(8,128)}, ...), condition=%wide.wide.region_6.7_spmd.clone, body=%wide.wide.region_4.6_spmd.clone.sunk | while | flops 678300160 | bytes 20476252 | solution.py:59
  126.8 2.7 fusion.31
  129.8 3.0 convolution_add_fusion.3
  138.4 2.7 fusion.31
  141.4 3.4 convolution_add_fusion.3
  150.4 2.7 fusion.31
  153.4 3.4 convolution_add_fusion.3
  162.5 2.7 fusion.31
  165.5 3.4 convolution_add_fusion.3
  174.6 2.7 fusion.31
  177.6 3.4 convolution_add_fusion.3
  186.6 2.7 fusion.31
  189.6 3.4 convolution_add_fusion.3
  198.7 2.7 fusion.31
  201.7 3.4 convolution_add_fusion.3
  210.8 2.7 fusion.31
  213.8 3.4 convolution_add_fusion.3
  218.4 113.9 %pmax.7 = f32[512,5]{1,0:T(8,128)S(1)} all-reduce(f32[512,5]{1,0:T(8,128)S(1)} %log_add_fusion), channel_id=1, replica_groups=mesh['ctx'=32,'grp'=8] {'ctx'}, use_global_device_ids=true, to_apply=%region_7.8 | all-reduce | flops 2560 | bytes 20480 | tf_op jit(solution)/shard_map/pmax | solution.py:63
  338.8 2.8 copy.28
  344.2 232.7 %reduce-scatter.5.cloned.1.call-done = f32[16,5]{1,0:T(8,128)} async-done(((f32[512,5]{1,0:T(8,128)}), f32[16,5]{1,0:T(8,128)}) %reduce-scatter.5.cloned.1.call-update) | async-done | bytes 336 | tf_op jit(solution)/shard_map/reduce_scatter | solution.py:68
  576.9 219.2 %reduce-scatter.3.cloned.1.call-done = f32[16,640]{1,0:T(8,128)} async-done(((f32[512,640]{1,0:T(8,128)}), f32[16,640]{1,0:T(8,128)}) %reduce-scatter.3.cloned.1.call-update) | async-done | bytes 40976 | tf_op jit(solution)/shard_map/reduce_scatter | solution.py:67
  797.6 14.5 %all_to_all.19 = bf16[8,2,640]{2,1,0:T(2,128)(2,1)S(1)} all-to-all(bf16[8,2,640]{2,1,0:T(2,128)(2,1)S(1)} %all_to_all.14), channel_id=1, replica_groups=mesh['ctx'=32,'grp'=8] {'grp'}, dimensions={0} | all-to-all | bytes 40960 | tf_op jit(solution)/shard_map/all_to_all | solution.py:71
  (260 shorter events, 130.5 us)
Async XLA Ops:
  6.5 570.4 %reduce-scatter.5.cloned.1.call-start = ((), (), s32[]{:S(2)}) async-start(), calls=%async_computation.4 | async-start | bytes 270336 | tf_op jit(solution)/shard_map/reduce_scatter | solution.py:68
  56.7 2.2 copy-start.4
  65.3 2.2 copy-start.4
  73.9 2.2 copy-start.4
  108.4 2.2 copy-start.4
  126.7 2.9 copy-start.1
  129.8 3.0 copy-start.2
  138.3 2.9 copy-start.1
  141.4 3.4 copy-start.2
  150.4 2.9 copy-start.1
  153.4 3.4 copy-start.2
  162.5 2.9 copy-start.1
  165.5 3.4 copy-start.2
  174.5 2.9 copy-start.1
  177.6 3.4 copy-start.2
  186.6 2.9 copy-start.1
  189.6 3.4 copy-start.2
  198.7 2.9 copy-start.1
  201.7 3.4 copy-start.2
  210.7 2.9 copy-start.1
  213.8 3.4 copy-start.2
  217.2 116.0 %copy-start.3 = (f32[512,5]{1,0:T(8,128)S(1)}, f32[512,5]{1,0:T(8,128)}, u32[]{:S(2)}) copy-start(f32[512,5]{1,0:T(8,128)} %get-tuple-element.241) | copy-start | bytes 30724
  217.2 117.2 %copy-start = (f32[2560,128]{1,0:T(8,128)S(1)}, f32[2560,128]{1,0:T(8,128)}, u32[]{:S(2)}) copy-start(f32[2560,128]{1,0:T(8,128)} %get-tuple-element.240) | copy-start | bytes 3932164
  333.1 462.9 %reduce-scatter.3.cloned.1.call-start = ((), (), s32[]{:S(2)}) async-start(), calls=%async_computation.3 | async-start | bytes 1351680 | tf_op jit(solution)/shard_map/reduce_scatter | solution.py:67
  (28 other events, 37.5 us)
Sparse Core Ops, SparseCore 0:
  333.2 243.6 reduce-scatter.4
  581.2 214.8 reduce-scatter.2
where the time goes:
time: 821 us; the launch traced here: 820 us
  waiting for transfers between devices  452 us (55%)
  blocking collectives  171 us (21%)
  local copies, waits for them, and re-layouts  110 us (13%)
  matrix products  64.3 us (8%)
  between operations  13.5 us (2%)
    reduce_scatter x1, waiting for transfers between devices, per_device(): lax.psum_scatter(factor, 'ctx', scatter_dimension=0, tiled=True)  233 us
    reduce_scatter x1, waiting for transfers between devices, per_device(): lax.psum_scatter(scaled_out, 'ctx', scatter_dimension=0, tiled=True)  219 us
    pmax x1, blocking collectives, per_device(): global_top = lax.pmax(log_total, 'ctx')  114 us
    all_gather x1, blocking collectives, per_device(): whole = lax.all_gather(query, 'ctx', axis=0, tiled=True)  42.3 us
    dot_general x16, matrix products, scores_at(): jnp.einsum('id,td->it', query_group, key_block, preferred_element_type=jn...  37.4 us
    broadcast_in_dim x24, local copies, waits for them, and re-layouts, first_pass(): jnp.where(block_mask, scores, -jnp.inf)  29.5 us
    broadcast_in_dim x24, local copies, waits for them, and re-layouts, second_pass(): weights = jnp.where(block_mask, jnp.exp(scores - local_max[..., None]), 0.0)  29.5 us
    dot_general x8, matrix products, second_pass(): jnp.dot(rounded, value_block, preferred_element_type=jnp.float32)  26.9 us
  transfers between devices with their start and end apart: 2, of which 2 were waited for; matrix products, arithmetic and copies ran while one was open for 1% of the time, Pallas kernels for 0%

commit v1 on v0

v1 whole, which is shorter than its diff:
```python
import functools
import math

import jax
import jax.numpy as jnp
from jax import lax
from jax.experimental import pallas as pl
from jax.experimental.pallas import tpu as pltpu
from jax.sharding import PartitionSpec as P

HD = 128
QPK = 5
BLOCK = 128
LANES = 128
TILE = 256
CHUNK = 256
UNLISTED = -float(2**17)
SCALE = 1.0 / math.sqrt(HD)
EXP2_SCALE = SCALE / math.log(2.0)


def attend_kernel(q_ref, k_ref, v_ref, blocks_ref, out_ref, kp_ref, vp_ref, bias_ref, s_ref, m_ref, top_ref, sum_ref):
    rows = q_ref.shape[0]
    tokens = k_ref.shape[0]
    halves = rows // TILE
    tiles = halves * QPK
    chunks = tokens // CHUNK
    listed = blocks_ref[...]
    ids = lax.broadcasted_iota(jnp.int32, (LANES, rows), 0)
    hit = ids < 0
    for j in range(listed.shape[0]):
        hit = hit | (listed[j : j + 1, :] == ids)
    bias_ref[...] = jnp.where(hit, 0.0, UNLISTED).T.astype(jnp.bfloat16)
    kp_ref[:, :HD] = k_ref[...]
    token = lax.broadcasted_iota(jnp.int32, (tokens, LANES), 0) // BLOCK
    lane = lax.broadcasted_iota(jnp.int32, (tokens, LANES), 1)
    kp_ref[:, HD:] = jnp.where(token == lane, 1.0, 0.0).astype(jnp.bfloat16)
    vp_ref[:, :HD] = v_ref[...]
    vp_ref[:, HD:] = jnp.ones((tokens, LANES), jnp.bfloat16)
    top_ref[...] = jnp.zeros_like(top_ref)
    sum_ref[...] = jnp.ones_like(sum_ref)

    def place(i):
        head = i // halves
        return (
            pl.ds(pl.multiple_of((i % halves) * TILE, TILE), TILE),
            pl.ds(pl.multiple_of(head * HD, HD), HD),
            head,
        )

    def score_start(i):
        at, columns, head = place(i)
        return jnp.concatenate([q_ref[at, columns], bias_ref[at, :]], axis=1)

    def score_chunk(i, c, left, best):
        span = slice(c * CHUNK, (c + 1) * CHUNK)
        s = lax.dot_general(left, kp_ref[span, :], (((1,), (1,)), ((), ())), preferred_element_type=jnp.float32)
        s_ref[i % 2, :, span] = s
        for part in range(CHUNK // LANES):
            piece = s[:, part * LANES : (part + 1) * LANES]
            best = piece if best is None else jnp.maximum(best, piece)
        return best

    def score_end(i, best):
        m_ref[i % 2] = jnp.broadcast_to(jnp.max(best, axis=1, keepdims=True), (TILE, LANES))

    def value_chunk(i, c, best, total):
        span = slice(c * CHUNK, (c + 1) * CHUNK)
        s = s_ref[i % 2, :, span]
        p = jnp.exp2((s - jnp.concatenate([best] * (CHUNK // LANES), axis=1)) * EXP2_SCALE).astype(jnp.bfloat16)
        add = jnp.dot(p, vp_ref[span, :], preferred_element_type=jnp.float32)
        return add if total is None else total + add

    def value_end(i, best, total):
        at, columns, head = place(i)
        weight = total[:, HD:]
        out_ref[at, columns] = (total[:, :HD] / weight).astype(jnp.bfloat16)
        here = lax.broadcasted_iota(jnp.int32, (TILE, LANES), 1) == head
        top_ref[at, :] = jnp.where(here, best, top_ref[at, :])
        sum_ref[at, :] = jnp.where(here, weight, sum_ref[at, :])

    def step(i, with_score, with_value):
        best_now = total = None
        if with_score:
            left = score_start(i)
        if with_value:
            best_before = m_ref[(i - 1) % 2]
        for c in range(chunks):
            if with_score:
                best_now = score_chunk(i, c, left, best_now)
            if with_value:
                total = value_chunk(i - 1, c, best_before, total)
        if with_score:
            score_end(i, best_now)
        if with_value:
            value_end(i - 1, best_before, total)

    step(jnp.int32(0), True, False)

    @pl.loop(1, tiles)
    def _(i):
        step(i, True, True)

    step(jnp.int32(tiles), False, True)

    lse = top_ref[...] * SCALE + jnp.log(sum_ref[...])
    high = lse.astype(jnp.bfloat16).astype(jnp.float32)
    rest = lse - high
    middle = rest.astype(jnp.bfloat16).astype(jnp.float32)
    low = (rest - middle).astype(jnp.bfloat16).astype(jnp.float32)
    packed = high + pltpu.roll(middle, 8, 1) + pltpu.roll(low, 16, 1)
    out_ref[:, QPK * HD :] = packed.astype(jnp.bfloat16)


def attend(query, keys, values, blocks):
    rows = query.shape[0]
    tokens = keys.shape[0]
    width = QPK * HD
    return pl.pallas_call(
        attend_kernel,
        out_shape=jax.ShapeDtypeStruct((rows, width + LANES), jnp.bfloat16),
        in_specs=[pl.BlockSpec(memory_space=pltpu.VMEM)] * 4,
        out_specs=pl.BlockSpec(memory_space=pltpu.VMEM),
        scratch_shapes=[
            pltpu.VMEM((tokens, 2 * HD), jnp.bfloat16),
            pltpu.VMEM((tokens, 2 * HD), jnp.bfloat16),
            pltpu.VMEM((rows, LANES), jnp.bfloat16),
            pltpu.VMEM((2, TILE, tokens), jnp.float32),
            pltpu.VMEM((2, TILE, LANES), jnp.float32),
            pltpu.VMEM((rows, LANES), jnp.float32),
            pltpu.VMEM((rows, LANES), jnp.float32),
        ],
        compiler_params=pltpu.CompilerParams(vmem_limit_bytes=40 * 2**20),
        name="attend",
    )(query, keys, values, blocks)


def combine_kernel(parts_ref, out_ref):
    packed = parts_ref[:, :, QPK * HD :].astype(jnp.float32)
    lse = packed + pltpu.roll(packed, LANES - 8, 2) + pltpu.roll(packed, LANES - 16, 2)
    top = jnp.max(lse, axis=0, keepdims=True)
    factor = jnp.exp(lse - top)
    weight = jnp.sum(factor, axis=0)
    for head in range(QPK):
        columns = slice(head * HD, (head + 1) * HD)
        part = parts_ref[:, :, columns].astype(jnp.float32)
        total = jnp.sum(factor[:, :, head : head + 1] * part, axis=0)
        out_ref[:, columns] = (total / weight[:, head : head + 1]).astype(jnp.bfloat16)


def combine(parts):
    shards, rows, width = parts.shape
    return pl.pallas_call(
        combine_kernel,
        out_shape=jax.ShapeDtypeStruct((rows, QPK * HD), jnp.bfloat16),
        in_specs=[pl.BlockSpec(memory_space=pltpu.VMEM)],
        out_specs=pl.BlockSpec(memory_space=pltpu.VMEM),
        name="combine",
    )(parts)


def per_device(query, keys, values, blocks):
    shards = lax.axis_size("ctx")
    own_rows, width = query.shape
    whole = lax.all_to_all(jnp.broadcast_to(query[None], (shards, own_rows, width)), "ctx", split_axis=0, concat_axis=0)
    whole = whole.reshape(shards * own_rows, width)
    parts = attend(whole, keys, values, blocks[:, 0, :].T)
    parts = lax.all_to_all(parts.reshape(shards, own_rows, -1), "ctx", split_axis=0, concat_axis=0)
    finished = combine(parts)
    return lax.all_to_all(finished, "grp", split_axis=0, concat_axis=1, tiled=True)


def solution(mesh):
    placed = (P("ctx", "grp"), P("ctx", "grp"), P("ctx", "grp"), P(None, "ctx", None))
    return jax.shard_map(
        per_device, mesh=mesh, in_specs=placed, out_specs=P(("ctx", "grp"), None), check_vma=False
    )
```

time: 821 us -> 108 us (0.13)
  waiting for transfers between devices: 452 us -> 0 us
  local copies, waits for them, and re-layouts: 110 us -> 3.45 us
  blocking collectives: 171 us -> 68.5 us
  matrix products: 64.3 us -> 0 us
  Pallas kernels: 0 us -> 35.3 us
  between operations: 13.5 us -> 0.02 us
    reduce_scatter x2 -> x0, waiting for transfers between devices: 452 us -> none  [the longest x1 233 us: per_device(): lax.psum_scatter(factor, 'ctx', scatter_dimension=0, tiled=True)]
    pmax x1 -> x0, blocking collectives: 114 us -> none  [per_device(): global_top = lax.pmax(log_total, 'ctx')]
    broadcast_in_dim x67 -> x1, local copies, waits for them, and re-layouts: 87.7 us -> 0.87 us  [per_device(): jnp.broadcast_to(query[None], (shards, own_rows, width))]
    dot_general x24 -> x0, matrix products: 64.3 us -> none  [the longest x16 37.4 us: scores_at(): jnp.einsum('id,td->it', query_group, key_block, preferred_element_type=jn...]
    all_to_all x0 -> x2, blocking collectives: none -> 55.7 us  [the longest x1 30.4 us: per_device(): lax.all_to_all(jnp.broadcast_to(query[None], (shards, own_rows, width)),...]
    all_gather x1 -> x0, blocking collectives: 42.3 us -> none  [per_device(): whole = lax.all_gather(query, 'ctx', axis=0, tiled=True)]
    pallas_call x0 -> x2, Pallas kernels: none -> 35.3 us  [the longest x1 33 us: attend(): pl.pallas_call(attend_kernel, out_shape=jax.ShapeDtypeStruct((rows, width...]
  transfers between devices with their start and end apart: 2 -> 0, of which waited for: 2 -> 0; matrix products, arithmetic and copies ran while one was open for 1% -> 0% of each run, Pallas kernels for 0% -> 0%
where the time goes in v1:
time: 108 us; the launch traced here: 107 us
  blocking collectives  68.5 us (63%)
  Pallas kernels  35.3 us (33%)
  local copies, waits for them, and re-layouts  3.45 us (3%)
    pallas_call x1, Pallas kernels, attend(): pl.pallas_call(attend_kernel, out_shape=jax.ShapeDtypeStruct((rows, width...  33 us
    all_to_all x1, blocking collectives, per_device(): lax.all_to_all(jnp.broadcast_to(query[None], (shards, own_rows, width)),...  30.4 us
    all_to_all x1, blocking collectives, per_device(): lax.all_to_all(parts.reshape(shards, own_rows, -1), 'ctx', split_axis=0,...  25.3 us
    all_to_all x1, blocking collectives, per_device(): lax.all_to_all(finished, 'grp', split_axis=0, concat_axis=1, tiled=True)  12.8 us
    pallas_call x1, Pallas kernels, combine(): pl.pallas_call(combine_kernel, out_shape=jax.ShapeDtypeStruct((rows, QPK...  2.31 us

profile of v1, /device:TPU:1, one launch (start us, length us, event | category | flops | bytes accessed | tf_op | source)
XLA Modules:
  0.0 107.2 jit_solution(5345828191996249391)
XLA Ops:
  0.0 0.0 copy-start
  0.0 0.9 broadcast_in_dim.2
  0.9 0.0 copy-start.2
  0.9 30.4 %all_to_all.29 = bf16[32,16,640]{2,1,0:T(8,128)(2,1)S(1)} all-to-all(bf16[32,16,640]{2,1,0:T(8,128)(2,1)S(1)} %broadcast_in_dim.2), channel_id=1, replica_groups=mesh['ctx'=32,'grp'=8] {'ctx'}, dimensions={0} | all-to-all | bytes 1310720 | tf_op jit(solution)/shard_map/all_to_all | solution.py:165
  31.2 0.0 copy-done
  31.3 0.0 copy-done.2
  31.3 0.0 copy-start.1
  31.3 1.2 %copy-done.1 = bf16[4096,128]{1,0:T(8,128)(2,1)S(1)} copy-done((bf16[4096,128]{1,0:T(8,128)(2,1)S(1)}, bf16[4096,128]{1,0:T(8,128)(2,1)}, u32[]{:S(2)}) %copy-start.1) | copy-done | bytes 1048600
  32.5 33.0 %attend.1 = bf16[512,768]{1,0:T(8,128)(2,1)S(1)} custom-call(bf16[512,640]{1,0:T(8,128)(2,1)S(1)} %bitcast.9, bf16[4096,128]{1,0:T(8,128)(2,1)S(1)} %copy-done, bf16[4096,128]{1,0:T(8,128)(2,1)S(1)} %copy-done.1, s32[8,512]{1,0:T(8,128)S(1)} %bitcast.10), custom_call_target="tpu_custom_call" | custom-call | tf_op jit(solution)/shard_map/attend/pallas_call | solution.py:119
  65.4 25.3 %all_to_all.30.parts_ref = bf16[32,16,768]{2,1,0:T(8,128)(2,1)} all-to-all(bf16[32,16,768]{2,1,0:T(8,128)(2,1)S(1)} %bitcast.8), channel_id=1, replica_groups=mesh['ctx'=32,'grp'=8] {'ctx'}, dimensions={0} | all-to-all | bytes 1572864 | tf_op jit(solution)/shard_map/all_to_all | solution.py:168
  90.7 2.3 %combine.1 = bf16[16,640]{1,0:T(8,128)(2,1)} custom-call(bf16[32,16,768]{2,1,0:T(8,128)(2,1)} %all_to_all.30.parts_ref), custom_call_target="tpu_custom_call" | custom-call | tf_op jit(solution)/shard_map/combine/pallas_call | solution.py:153
  93.1 0.7 all_to_all.22
  93.8 12.8 %all_to_all.31 = bf16[8,2,640]{2,1,0:T(2,128)(2,1)S(1)} all-to-all(bf16[8,2,640]{2,1,0:T(2,128)(2,1)S(1)} %all_to_all.22), channel_id=1, replica_groups=mesh['ctx'=32,'grp'=8] {'grp'}, dimensions={0} | all-to-all | bytes 40960 | tf_op jit(solution)/shard_map/all_to_all | solution.py:170
  106.6 0.6 copy.7
Async XLA Ops:
  0.0 31.2 %copy-start = (bf16[4096,128]{1,0:T(8,128)(2,1)S(1)}, bf16[4096,128]{1,0:T(8,128)(2,1)}, u32[]{:S(2)}) copy-start(bf16[4096,128]{1,0:T(8,128)(2,1)} %k_ref.1) | copy-start | bytes 3145732
  0.9 30.4 %copy-start.2 = (s32[512,1,8]{0,2,1:T(8,128)S(1)}, s32[512,1,8]{0,2,1:T(8,128)}, u32[]{:S(2)}) copy-start(s32[512,1,8]{0,2,1:T(8,128)} %param.7) | copy-start | bytes 49156
  31.3 1.2 %copy-start.1 = (bf16[4096,128]{1,0:T(8,128)(2,1)S(1)}, bf16[4096,128]{1,0:T(8,128)(2,1)}, u32[]{:S(2)}) copy-start(bf16[4096,128]{1,0:T(8,128)(2,1)} %v_ref.1) | copy-start | bytes 3145732

commit v2 on v0

v2 whole, which is shorter than its diff:
```python
import math

import jax
import jax.numpy as jnp
from jax import lax
from jax.experimental import pallas as pl
from jax.experimental.pallas import tpu as pltpu
from jax.sharding import Mesh
from jax.sharding import PartitionSpec as P

HD = 128
QPK = 5
BLOCK = 128
DEPTH = 8
ACROSS = 4
LANES = 128
TILE_ROWS = 64
CHUNK = 512
SHIFTS = (0, 2, 1, 3)
UNLISTED = -float(2**17)
SCALE = 1.0 / math.sqrt(HD)
EXP2_SCALE = SCALE / math.log(2.0)


def prepare_kernel(x_ref, blocks_ref, k_ref, v_ref, bias_ref, kept_k_ref, kept_v_ref, hot_ref, arrived):
    copies = [
        pltpu.make_async_copy(k_ref, kept_k_ref, arrived.at[0]),
        pltpu.make_async_copy(v_ref, kept_v_ref, arrived.at[1]),
    ]
    for copy in copies:
        copy.start()
    shifts, rows, _ = bias_ref.shape
    listed = blocks_ref[...]
    total = listed.shape[1]
    own = total // (shifts * DEPTH)
    ids = lax.broadcasted_iota(jnp.int32, (LANES, total), 0)
    hit = ids < 0
    for j in range(listed.shape[0]):
        hit = hit | (listed[j : j + 1, :] == ids)
    bias = jnp.where(hit, 0.0, UNLISTED).T.astype(jnp.bfloat16)
    pieces = [bias[i * own : (i + 1) * own, :] for i in range(total // own)]
    for shift in range(shifts):
        source = lax.rem(x_ref[0] + (shifts - shift), shifts)
        for z in range(DEPTH):
            piece = pieces[z * shifts]
            for x in range(1, shifts):
                piece = jnp.where(source == x, pieces[z * shifts + x], piece)
            bias_ref[shift, z * own : (z + 1) * own, :] = piece
    lane = lax.broadcasted_iota(jnp.int32, (BLOCK, LANES), 1)
    for block in range(hot_ref.shape[0] // BLOCK):
        hot_ref[block * BLOCK : (block + 1) * BLOCK, :] = jnp.where(lane == block, 1.0, 0.0).astype(jnp.bfloat16)
    for copy in copies:
        copy.wait()


def prepare(x, blocks, keys, values, across):
    rows = blocks.shape[1] // across
    tokens = keys.shape[0]
    whole = pl.BlockSpec(memory_space=pltpu.VMEM)
    return pl.pallas_call(
        prepare_kernel,
        out_shape=(
            jax.ShapeDtypeStruct((across, rows, LANES), jnp.bfloat16),
            jax.ShapeDtypeStruct(keys.shape, jnp.bfloat16),
            jax.ShapeDtypeStruct(values.shape, jnp.bfloat16),
            jax.ShapeDtypeStruct((tokens, LANES), jnp.bfloat16),
        ),
        in_specs=[
            pl.BlockSpec(memory_space=pltpu.SMEM),
            whole,
            pl.BlockSpec(memory_space=pltpu.HBM),
            pl.BlockSpec(memory_space=pltpu.HBM),
        ],
        out_specs=(whole, whole, whole, whole),
        scratch_shapes=[pltpu.SemaphoreType.DMA((2,))],
        compiler_params=pltpu.CompilerParams(vmem_limit_bytes=8 * 2**20),
        cost_estimate=pl.CostEstimate(flops=2**20, transcendentals=0, bytes_accessed=4 * 2**20),
        name="prepare",
    )(x, blocks, keys, values)


def pack_lse(lse):
    high = lse.astype(jnp.bfloat16).astype(jnp.float32)
    rest = lse - high
    middle = rest.astype(jnp.bfloat16).astype(jnp.float32)
    low = (rest - middle).astype(jnp.bfloat16).astype(jnp.float32)
    return (high + pltpu.roll(middle, 8, 1) + pltpu.roll(low, 16, 1)).astype(jnp.bfloat16)


def attend_kernel(shift, q_ref, bias_ref, k_ref, hot_ref, v_ref, out_ref, s_ref):
    rows = q_ref.shape[0]
    tokens = k_ref.shape[0]
    tiles = rows // TILE_ROWS
    height = TILE_ROWS * QPK
    chunks = tokens // CHUNK
    ones = jnp.ones((CHUNK, LANES), jnp.bfloat16)
    lefts, bests, tops, totals = {}, {}, {}, {}

    def score_start(i):
        at = slice(i * TILE_ROWS, (i + 1) * TILE_ROWS)
        bias = bias_ref[shift, at, :]
        query = jnp.concatenate([q_ref[at, h * HD : (h + 1) * HD] for h in range(QPK)], axis=0)
        lefts[i] = jnp.concatenate([query, jnp.concatenate([bias] * QPK, axis=0)], axis=1)

    def score_chunk(i, c):
        span = slice(c * CHUNK, (c + 1) * CHUNK)
        right = jnp.concatenate([k_ref[span, :], hot_ref[span, :]], axis=1)
        s = lax.dot_general(lefts[i], right, (((1,), (1,)), ((), ())), preferred_element_type=jnp.float32)
        s_ref[i % 2, :, span] = s
        best = bests.get(i)
        for part in range(CHUNK // LANES):
            piece = s[:, part * LANES : (part + 1) * LANES]
            best = piece if best is None else jnp.maximum(best, piece)
        bests[i] = best

    def score_end(i):
        tops[i] = jnp.broadcast_to(jnp.max(bests[i], axis=1, keepdims=True), (height, LANES))

    def value_chunk(i, c):
        span = slice(c * CHUNK, (c + 1) * CHUNK)
        s = s_ref[i % 2, :, span]
        top = jnp.concatenate([tops[i]] * (CHUNK // LANES), axis=1)
        p = jnp.exp2((s - top) * EXP2_SCALE).astype(jnp.bfloat16)
        add = jnp.dot(p, jnp.concatenate([v_ref[span, :], ones], axis=1), preferred_element_type=jnp.float32)
        totals[i] = totals[i] + add if i in totals else add

    def value_end(i):
        at = slice(i * TILE_ROWS, (i + 1) * TILE_ROWS)
        lane = lax.broadcasted_iota(jnp.int32, (TILE_ROWS, LANES), 1)
        top = jnp.zeros((TILE_ROWS, LANES), jnp.float32)
        weight = jnp.ones((TILE_ROWS, LANES), jnp.float32)
        for h in range(QPK):
            span = slice(h * TILE_ROWS, (h + 1) * TILE_ROWS)
            mass = totals[i][span, HD:]
            out_ref[at, h * HD : (h + 1) * HD] = (totals[i][span, :HD] / mass).astype(jnp.bfloat16)
            top = jnp.where(lane == h, tops[i][span, :], top)
            weight = jnp.where(lane == h, mass, weight)
        out_ref[at, QPK * HD :] = pack_lse(top * SCALE + jnp.log(weight))

    for i in range(tiles + 1):
        if i < tiles:
            score_start(i)
        for c in range(chunks):
            if i < tiles:
                score_chunk(i, c)
            if i > 0:
                value_chunk(i - 1, c)
        if i < tiles:
            score_end(i)
        if i > 0:
            value_end(i - 1)


def group(shift, query, bias, keys, hot, values):
    rows = query.shape[0]
    tokens = keys.shape[0]
    width = QPK * HD
    return pl.pallas_call(
        lambda *refs: attend_kernel(shift, *refs),
        out_shape=jax.ShapeDtypeStruct((rows, width + LANES), jnp.bfloat16),
        in_specs=[pl.BlockSpec(memory_space=pltpu.VMEM)] * 5,
        out_specs=pl.BlockSpec(memory_space=pltpu.VMEM),
        scratch_shapes=[pltpu.VMEM((2, TILE_ROWS * QPK, tokens), jnp.float32)],
        compiler_params=pltpu.CompilerParams(vmem_limit_bytes=20 * 2**20),
        cost_estimate=pl.CostEstimate(
            flops=8 * rows * QPK * tokens * HD, transcendentals=rows * QPK * tokens, bytes_accessed=2 * 2**20
        ),
        name="attend",
    )(query, bias, keys, hot, values)


def unpack_lse(packed):
    packed = packed.astype(jnp.float32)
    axis = packed.ndim - 1
    return packed + pltpu.roll(packed, LANES - 8, axis) + pltpu.roll(packed, LANES - 16, axis)


def merge_kernel(*refs):
    parts, out_ref = refs[:-1], refs[-1]
    width = QPK * HD
    lses = [unpack_lse(ref[:, width:]) for ref in parts]
    top = lses[0]
    for lse in lses[1:]:
        top = jnp.maximum(top, lse)
    factors = [jnp.exp(lse - top) for lse in lses]
    weight = factors[0]
    for factor in factors[1:]:
        weight = weight + factor
    share = [factor / weight for factor in factors]
    for h in range(QPK):
        columns = slice(h * HD, (h + 1) * HD)
        total = None
        for ref, factor in zip(parts, share):
            term = factor[:, h : h + 1] * ref[:, columns].astype(jnp.float32)
            total = term if total is None else total + term
        out_ref[:, columns] = total.astype(jnp.bfloat16)
    lane = lax.broadcasted_iota(jnp.int32, top.shape, 1)
    out_ref[:, width:] = pack_lse(jnp.where(lane < QPK, top + jnp.log(weight), 0.0))


def merge(parts):
    return pl.pallas_call(
        merge_kernel,
        out_shape=jax.ShapeDtypeStruct(parts[0].shape, jnp.bfloat16),
        in_specs=[pl.BlockSpec(memory_space=pltpu.VMEM)] * len(parts),
        out_specs=pl.BlockSpec(memory_space=pltpu.VMEM),
        compiler_params=pltpu.CompilerParams(vmem_limit_bytes=8 * 2**20),
        name="merge",
    )(*parts)


def finish_kernel(parts_ref, out_ref):
    width = QPK * HD
    lse = unpack_lse(parts_ref[:, :, width:])
    top = jnp.max(lse, axis=0, keepdims=True)
    factor = jnp.exp(lse - top)
    weight = jnp.sum(factor, axis=0)
    rows, total_width = out_ref.shape
    for h in range(QPK):
        part = parts_ref[:, :, h * HD : (h + 1) * HD].astype(jnp.float32)
        total = jnp.sum(factor[:, :, h : h + 1] * part, axis=0)
        done = (total / weight[:, h : h + 1]).astype(jnp.bfloat16)
        for g in range(total_width // width):
            out_ref[:, g * width + h * HD : g * width + (h + 1) * HD] = done[g * rows : (g + 1) * rows, :]


def finish(parts, rows):
    shards, grouped, wide = parts.shape
    return pl.pallas_call(
        finish_kernel,
        out_shape=jax.ShapeDtypeStruct((rows, grouped // rows * QPK * HD), jnp.bfloat16),
        in_specs=[pl.BlockSpec(memory_space=pltpu.VMEM)],
        out_specs=pl.BlockSpec(memory_space=pltpu.VMEM),
        compiler_params=pltpu.CompilerParams(vmem_limit_bytes=8 * 2**20),
        name="finish",
    )(parts)


def per_device(query, keys, values, blocks):
    depth, across, groups = lax.axis_size("z"), lax.axis_size("x"), lax.axis_size("grp")
    own_rows, width = query.shape
    rows = depth * own_rows
    x = lax.axis_index("x").reshape(1)
    bias, keys, values, hot = prepare(x, blocks[:, 0, :].T, keys, values, across)
    wide = jnp.broadcast_to(query[None], (depth, own_rows, width))
    column = lax.all_to_all(wide, "z", split_axis=0, concat_axis=0).reshape(rows, width)

    def move(array, shift):
        return lax.ppermute(array, "x", [(i, (i + shift) % across) for i in range(across)])

    queries = {shift: move(column, shift) if shift else column for shift in SHIFTS}
    parts = []
    for shift in SHIFTS:
        part = group(shift, queries[shift], bias, keys, hot, values)
        parts.append(move(part, across - shift) if shift else part)
    merged = merge(parts)
    share = own_rows // groups
    pieces = lax.all_to_all(merged.reshape(depth * groups, share, -1), ("z", "grp"), split_axis=0, concat_axis=0)
    return finish(pieces.reshape(depth, own_rows, -1), share)


def solution(mesh):
    split = Mesh(mesh.devices.reshape(DEPTH, ACROSS, -1), ("z", "x", "grp"))
    ctx = ("z", "x")
    placed = (P(ctx, "grp"), P(ctx, "grp"), P(ctx, "grp"), P(None, ctx, None))
    return jax.shard_map(
        per_device, mesh=split, in_specs=placed, out_specs=P(("z", "x", "grp"), None), check_vma=False
    )
```

time: 821 us -> 68.7 us (0.08)
  waiting for transfers between devices: 452 us -> 2.66 us
  blocking collectives: 171 us -> 40.2 us
  local copies, waits for them, and re-layouts: 110 us -> 3.35 us
  matrix products: 64.3 us -> 0 us
  Pallas kernels: 0 us -> 14.7 us
  between operations: 13.5 us -> 0.09 us
    reduce_scatter x2 -> x0, waiting for transfers between devices: 452 us -> none  [the longest x1 233 us: per_device(): lax.psum_scatter(factor, 'ctx', scatter_dimension=0, tiled=True)]
    pmax x1 -> x0, blocking collectives: 114 us -> none  [per_device(): global_top = lax.pmax(log_total, 'ctx')]
    broadcast_in_dim x67 -> x1, local copies, waits for them, and re-layouts: 87.7 us -> 0.74 us  [per_device(): wide = jnp.broadcast_to(query[None], (depth, own_rows, width))]
    dot_general x24 -> x0, matrix products: 64.3 us -> none  [the longest x16 37.4 us: scores_at(): jnp.einsum('id,td->it', query_group, key_block, preferred_element_type=jn...]
    all_gather x1 -> x0, blocking collectives: 42.3 us -> none  [per_device(): whole = lax.all_gather(query, 'ctx', axis=0, tiled=True)]
    all_to_all x1 -> x2, blocking collectives: 14.5 us -> 40.2 us  [the longest x1 23.3 us: per_device(): lax.all_to_all(merged.reshape(depth * groups, share, -1), ('z', 'grp'), s...]
    pallas_call x0 -> x7, Pallas kernels: none -> 14.7 us  [the longest x4 12.7 us: group(): pl.pallas_call(lambda *refs: attend_kernel(shift, *refs), out_shape=jax.S...]
  transfers between devices with their start and end apart: 2 -> 6, of which waited for: 2 -> 2; matrix products, arithmetic and copies ran while one was open for 1% -> 0% of each run, Pallas kernels for 0% -> 19%
where the time goes in v2:
time: 68.7 us; the launch traced here: 68.3 us
  blocking collectives  40.2 us (59%)
  Pallas kernels  14.7 us (21%)
  starting transfers between devices  7.3 us (11%)
  local copies, waits for them, and re-layouts  3.35 us (5%)
  waiting for transfers between devices  2.66 us (4%)
    all_to_all x1, blocking collectives, per_device(): lax.all_to_all(merged.reshape(depth * groups, share, -1), ('z', 'grp'), s...  23.3 us
    all_to_all x1, blocking collectives, per_device(): lax.all_to_all(wide, 'z', split_axis=0, concat_axis=0).reshape(rows, width)  17 us
    pallas_call x4, Pallas kernels, group(): pl.pallas_call(lambda *refs: attend_kernel(shift, *refs), out_shape=jax.S...  12.7 us
    ppermute x6, starting transfers between devices, move(): lax.ppermute(array, 'x', [(i, (i + shift) % across) for i in range(across)])  7.3 us
    ppermute x6, waiting for transfers between devices, move(): lax.ppermute(array, 'x', [(i, (i + shift) % across) for i in range(across)])  2.66 us
    unnamed x6, local copies, waits for them, and re-layouts  2.46 us
  transfers between devices with their start and end apart: 6, of which 2 were waited for; matrix products, arithmetic and copies ran while one was open for 0% of the time, Pallas kernels for 19%

profile of v2, /device:TPU:1, one launch (start us, length us, event | category | flops | bytes accessed | tf_op | source)
XLA Modules:
  0.0 68.3 jit_solution(9130079540290919881)
XLA Ops:
  0.0 0.7 %broadcast_in_dim.2 = bf16[8,16,640]{2,1,0:T(8,128)(2,1)S(1)} broadcast(bf16[16,640]{1,0:T(8,128)(2,1)} %param.4), dimensions={1,2} | broadcast | bytes 184320 | tf_op jit(solution)/shard_map/broadcast_in_dim | solution.py:245
  0.7 0.0 copy-start.2
  0.8 17.0 %all_to_all.10 = bf16[8,16,640]{2,1,0:T(8,128)(2,1)S(1)} all-to-all(bf16[8,16,640]{2,1,0:T(8,128)(2,1)S(1)} %broadcast_in_dim.2), channel_id=1, replica_groups=mesh['z'=8,'x'=4,'grp'=8] {'z'}, dimensions={0} | all-to-all | bytes 327680 | tf_op jit(solution)/shard_map/all_to_all | solution.py:246
  17.7 2.7 %collective-permute-start = (bf16[128,640]{1,0:T(8,128)(2,1)S(1)}, bf16[128,640]{1,0:T(8,128)(2,1)S(1)}, u32[]{:S(2)}, u32[]{:S(2)}) collective-permute-start(bf16[128,640]{1,0:T(8,128)(2,1)S(1)} %bitcast.5), channel_id=1, source_target_pairs={{0,16},{8,24},{16,0},{24,8},{1,17},{9,25},{17,1},{25,9},{2,18},{10... | collective-permute-start | bytes 491528 | tf_op jit(solution)/shard_map/ppermute | solution.py:249
  20.5 1.2 %copy-done = bf16[4096,128]{1,0:T(8,128)(2,1)S(1)} copy-done((bf16[4096,128]{1,0:T(8,128)(2,1)S(1)}, bf16[4096,128]{1,0:T(8,128)(2,1)}, u32[]{:S(2)}) %copy-start) | copy-done | bytes 1048600
  21.7 1.2 %copy-done.1 = bf16[4096,128]{1,0:T(8,128)(2,1)S(1)} copy-done((bf16[4096,128]{1,0:T(8,128)(2,1)S(1)}, bf16[4096,128]{1,0:T(8,128)(2,1)}, u32[]{:S(2)}) %copy-start.1) | copy-done | bytes 1048600
  22.9 0.5 prepare.1
  23.5 0.9 %collective-permute-start.4 = (bf16[128,640]{1,0:T(8,128)(2,1)S(1)}, bf16[128,640]{1,0:T(8,128)(2,1)S(1)}, u32[]{:S(2)}, u32[]{:S(2)}) collective-permute-start(bf16[128,640]{1,0:T(8,128)(2,1)S(1)} %bitcast.6), channel_id=1, source_target_pairs={{0,24},{8,0},{16,8},{24,16},{1,25},{9,1},{17,9},{25,17},{2,26},{10... | collective-permute-start | bytes 491528 | tf_op jit(solution)/shard_map/ppermute | solution.py:249
  24.4 0.6 collective-permute-start.2
  25.0 0.0 collective-permute-done.refs_0_
  25.0 3.2 %attend.5 = bf16[128,768]{1,0:T(8,128)(2,1)S(1)} custom-call(bf16[128,640]{1,0:T(8,128)(2,1)S(1)} %collective-permute-done.refs_0_, bf16[4,128,128]{2,1,0:T(8,128)(2,1)S(1)} %get-tuple-element.9.refs_1_, bf16[4096,128]{1,0:T(8,128)(2,1)S(1)} %get-tuple-element.10.refs_2_, bf16[4096,128]{1,0:T(8,128)(2,1)S(1)} %get-tuple-element.11.refs_3_, ...), custom_call_target="tpu_custom_call" | custom-call | flops 2684354560 | bytes 2097152 | tf_op jit(solution)/shard_map/attend/pallas_call | solution.py:158
  28.2 1.2 %collective-permute-start.1 = (bf16[128,768]{1,0:T(8,128)(2,1)S(1)}, bf16[128,768]{1,0:T(8,128)(2,1)S(1)}, u32[]{:S(2)}, u32[]{:S(2)}) collective-permute-start(bf16[128,768]{1,0:T(8,128)(2,1)S(1)} %attend.5), channel_id=1, source_target_pairs={{0,16},{8,24},{16,0},{24,8},{1,17},{9,25},{17,1},{25,9},{2,18},{10... | collective-permute-start | bytes 589832 | tf_op jit(solution)/shard_map/ppermute | solution.py:249
  29.4 0.4 collective-permute-done.2.refs_0_
  29.8 3.2 %attend.6 = bf16[128,768]{1,0:T(8,128)(2,1)S(1)} custom-call(bf16[128,640]{1,0:T(8,128)(2,1)S(1)} %collective-permute-done.2.refs_0_, bf16[4,128,128]{2,1,0:T(8,128)(2,1)S(1)} %get-tuple-element.9.refs_1_, bf16[4096,128]{1,0:T(8,128)(2,1)S(1)} %get-tuple-element.10.refs_2_, bf16[4096,128]{1,0:T(8,128)(2,1)S(1)} %get-tuple-element.11.refs_3_, ...), custom_call_target="tpu_custom_call" | custom-call | flops 2684354560 | bytes 2097152 | tf_op jit(solution)/shard_map/attend/pallas_call | solution.py:158
  33.0 1.5 %collective-permute-start.3 = (bf16[128,768]{1,0:T(8,128)(2,1)S(1)}, bf16[128,768]{1,0:T(8,128)(2,1)S(1)}, u32[]{:S(2)}, u32[]{:S(2)}) collective-permute-start(bf16[128,768]{1,0:T(8,128)(2,1)S(1)} %attend.6), channel_id=1, source_target_pairs={{0,24},{8,0},{16,8},{24,16},{1,25},{9,1},{17,9},{25,17},{2,26},{10... | collective-permute-start | bytes 589832 | tf_op jit(solution)/shard_map/ppermute | solution.py:249
  34.4 3.2 %attend.7 = bf16[128,768]{1,0:T(8,128)(2,1)S(1)} custom-call(bf16[128,640]{1,0:T(8,128)(2,1)S(1)} %collective-permute-done.4.refs_0_, bf16[4,128,128]{2,1,0:T(8,128)(2,1)S(1)} %get-tuple-element.9.refs_1_, bf16[4096,128]{1,0:T(8,128)(2,1)S(1)} %get-tuple-element.10.refs_2_, bf16[4096,128]{1,0:T(8,128)(2,1)S(1)} %get-tuple-element.11.refs_3_, ...), custom_call_target="tpu_custom_call" | custom-call | flops 2684354560 | bytes 2097152 | tf_op jit(solution)/shard_map/attend/pallas_call | solution.py:158
  37.6 0.3 collective-permute-start.5
  37.9 3.2 %attend.4.refs_0_ = bf16[128,768]{1,0:T(8,128)(2,1)S(1)} custom-call(bf16[128,640]{1,0:T(8,128)(2,1)S(1)} %bitcast.8, bf16[4,128,128]{2,1,0:T(8,128)(2,1)S(1)} %get-tuple-element.9.refs_1_, bf16[4096,128]{1,0:T(8,128)(2,1)S(1)} %get-tuple-element.10.refs_2_, bf16[4096,128]{1,0:T(8,128)(2,1)S(1)} %get-tuple-element.11.refs_3_, ...), custom_call_target="tpu_custom_call" | custom-call | flops 2684354560 | bytes 2097152 | tf_op jit(solution)/shard_map/attend/pallas_call | solution.py:158
  41.1 2.3 %collective-permute-done.5.refs_3_ = bf16[128,768]{1,0:T(8,128)(2,1)S(1)} collective-permute-done((bf16[128,768]{1,0:T(8,128)(2,1)S(1)}, bf16[128,768]{1,0:T(8,128)(2,1)S(1)}, u32[]{:S(2)}, u32[]{:S(2)}) %collective-permute-start.5) | collective-permute-done | bytes 196640 | tf_op jit(solution)/shard_map/ppermute | solution.py:249
  43.4 0.6 merge.1
  44.0 0.1 reshape.15
  44.1 23.3 %all_to_all.11 = bf16[64,2,768]{2,1,0:T(2,128)(2,1)S(1)} all-to-all(bf16[64,2,768]{2,1,0:T(2,128)(2,1)S(1)} %reshape.15), channel_id=1, replica_groups=mesh['z'=8,'x'=4,'grp'=8] {'z','grp'}, dimensions={0} | all-to-all | bytes 393216 | tf_op jit(solution)/shard_map/all_to_all | solution.py:258
  67.4 0.1 reshape.16.parts_ref
  67.5 0.9 %finish.1 = bf16[2,5120]{1,0:T(2,128)(2,1)} custom-call(bf16[8,16,768]{2,1,0:T(8,128)(2,1)S(1)} %reshape.16.parts_ref), custom_call_target="tpu_custom_call" | custom-call | tf_op jit(solution)/shard_map/finish/pallas_call | solution.py:229
  (6 shorter events, 0.0 us)
Async XLA Ops:
  0.7 19.7 %copy-start.2 = (s32[512,1,8]{0,2,1:T(8,128)S(1)}, s32[512,1,8]{0,2,1:T(8,128)}, u32[]{:S(2)}) copy-start(s32[512,1,8]{0,2,1:T(8,128)} %param.7) | copy-start | bytes 49156
  17.7 7.3 %collective-permute-start = (bf16[128,640]{1,0:T(8,128)(2,1)S(1)}, bf16[128,640]{1,0:T(8,128)(2,1)S(1)}, u32[]{:S(2)}, u32[]{:S(2)}) collective-permute-start(bf16[128,640]{1,0:T(8,128)(2,1)S(1)} %bitcast.5), channel_id=1, source_target_pairs={{0,16},{8,24},{16,0},{24,8},{1,17},{9,25},{17,1},{25,9},{2,18},{10... | collective-permute-start | bytes 491528 | tf_op jit(solution)/shard_map/ppermute | solution.py:249
  20.5 1.2 %copy-start = (bf16[4096,128]{1,0:T(8,128)(2,1)S(1)}, bf16[4096,128]{1,0:T(8,128)(2,1)}, u32[]{:S(2)}) copy-start(bf16[4096,128]{1,0:T(8,128)(2,1)} %k_ref.1) | copy-start | bytes 3145732
  21.7 1.2 %copy-start.1 = (bf16[4096,128]{1,0:T(8,128)(2,1)S(1)}, bf16[4096,128]{1,0:T(8,128)(2,1)}, u32[]{:S(2)}) copy-start(bf16[4096,128]{1,0:T(8,128)(2,1)} %v_ref.1) | copy-start | bytes 3145732
  23.5 11.0 %collective-permute-start.4 = (bf16[128,640]{1,0:T(8,128)(2,1)S(1)}, bf16[128,640]{1,0:T(8,128)(2,1)S(1)}, u32[]{:S(2)}, u32[]{:S(2)}) collective-permute-start(bf16[128,640]{1,0:T(8,128)(2,1)S(1)} %bitcast.6), channel_id=1, source_target_pairs={{0,24},{8,0},{16,8},{24,16},{1,25},{9,1},{17,9},{25,17},{2,26},{10... | collective-permute-start | bytes 491528 | tf_op jit(solution)/shard_map/ppermute | solution.py:249
  24.4 5.4 %collective-permute-start.2 = (bf16[128,640]{1,0:T(8,128)(2,1)S(1)}, bf16[128,640]{1,0:T(8,128)(2,1)S(1)}, u32[]{:S(2)}, u32[]{:S(2)}) collective-permute-start(bf16[128,640]{1,0:T(8,128)(2,1)S(1)} %bitcast.7), channel_id=1, source_target_pairs={{0,8},{8,16},{16,24},{24,0},{1,9},{9,17},{17,25},{25,1},{2,10},{10... | collective-permute-start | bytes 491528 | tf_op jit(solution)/shard_map/ppermute | solution.py:249
  28.2 12.9 %collective-permute-start.1 = (bf16[128,768]{1,0:T(8,128)(2,1)S(1)}, bf16[128,768]{1,0:T(8,128)(2,1)S(1)}, u32[]{:S(2)}, u32[]{:S(2)}) collective-permute-start(bf16[128,768]{1,0:T(8,128)(2,1)S(1)} %attend.5), channel_id=1, source_target_pairs={{0,16},{8,24},{16,0},{24,8},{1,17},{9,25},{17,1},{25,9},{2,18},{10... | collective-permute-start | bytes 589832 | tf_op jit(solution)/shard_map/ppermute | solution.py:249
  33.0 8.2 %collective-permute-start.3 = (bf16[128,768]{1,0:T(8,128)(2,1)S(1)}, bf16[128,768]{1,0:T(8,128)(2,1)S(1)}, u32[]{:S(2)}, u32[]{:S(2)}) collective-permute-start(bf16[128,768]{1,0:T(8,128)(2,1)S(1)} %attend.6), channel_id=1, source_target_pairs={{0,24},{8,0},{16,8},{24,16},{1,25},{9,1},{17,9},{25,17},{2,26},{10... | collective-permute-start | bytes 589832 | tf_op jit(solution)/shard_map/ppermute | solution.py:249
  37.6 5.8 %collective-permute-start.5 = (bf16[128,768]{1,0:T(8,128)(2,1)S(1)}, bf16[128,768]{1,0:T(8,128)(2,1)S(1)}, u32[]{:S(2)}, u32[]{:S(2)}) collective-permute-start(bf16[128,768]{1,0:T(8,128)(2,1)S(1)} %attend.7), channel_id=1, source_target_pairs={{0,8},{8,16},{16,24},{24,0},{1,9},{9,17},{17,25},{25,1},{2,10},{10... | collective-permute-start | bytes 589832 | tf_op jit(solution)/shard_map/ppermute | solution.py:249

commit v3 on v2

--- a/solution.py
+++ b/solution.py
@@ -76,7 +76,12 @@
         compiler_params=pltpu.CompilerParams(vmem_limit_bytes=8 * 2**20),
         cost_estimate=pl.CostEstimate(flops=2**20, transcendentals=0, bytes_accessed=4 * 2**20),
         name="prepare",
-    )(x, blocks, keys, values)
+    )(
+        x,
+        blocks,
+        pltpu.with_memory_space_constraint(keys, pltpu.HBM),
+        pltpu.with_memory_space_constraint(values, pltpu.HBM),
+    )
 
 
 def pack_lse(lse):

time: 68.7 us -> 68.6 us (level)
  local copies, waits for them, and re-layouts: 3.35 us -> 0.9 us
  starting transfers between devices: 7.3 us -> 8.73 us
  Pallas kernels: 14.7 us -> 15.7 us
  waiting for transfers between devices: 2.66 us -> 1.94 us
  blocking collectives: 40.2 us -> 40.9 us
    unnamed x6 -> x2, local copies, waits for them, and re-layouts: 2.46 us -> 0.01 us
    ppermute x6, starting transfers between devices: 7.3 us -> 8.73 us  [move(): lax.ppermute(array, 'x', [(i, (i + shift) % across) for i in range(across)])]
    pallas_call x1, Pallas kernels: 0.54 us -> 1.56 us  [prepare(): pl.pallas_call(prepare_kernel, out_shape=(jax.ShapeDtypeStruct((across, r...]
    ppermute x6, waiting for transfers between devices: 2.66 us -> 1.94 us  [move(): lax.ppermute(array, 'x', [(i, (i + shift) % across) for i in range(across)])]
    all_to_all x1, blocking collectives: 23.3 us -> 24 us  [per_device(): lax.all_to_all(merged.reshape(depth * groups, share, -1), ('z', 'grp'), s...]
  transfers between devices with their start and end apart: 6 -> 6, of which waited for: 2 -> 1; matrix products, arithmetic and copies ran while one was open for 0% -> 0% of each run, Pallas kernels for 19% -> 21%
where the time goes in v3:
time: 68.6 us; the launch traced here: 68.3 us
  blocking collectives  40.9 us (60%)
  Pallas kernels  15.7 us (23%)
  starting transfers between devices  8.73 us (13%)
  waiting for transfers between devices  1.94 us (3%)
  local copies, waits for them, and re-layouts  0.9 us (1%)
    all_to_all x1, blocking collectives, per_device(): lax.all_to_all(merged.reshape(depth * groups, share, -1), ('z', 'grp'), s...  24 us
    all_to_all x1, blocking collectives, per_device(): lax.all_to_all(wide, 'z', split_axis=0, concat_axis=0).reshape(rows, width)  17 us
    pallas_call x4, Pallas kernels, group(): pl.pallas_call(lambda *refs: attend_kernel(shift, *refs), out_shape=jax.S...  12.7 us
    ppermute x6, starting transfers between devices, move(): lax.ppermute(array, 'x', [(i, (i + shift) % across) for i in range(across)])  8.73 us
    ppermute x6, waiting for transfers between devices, move(): lax.ppermute(array, 'x', [(i, (i + shift) % across) for i in range(across)])  1.94 us
    pallas_call x1, Pallas kernels, prepare(): pl.pallas_call(prepare_kernel, out_shape=(jax.ShapeDtypeStruct((across, r...  1.56 us
  transfers between devices with their start and end apart: 6, of which 1 were waited for; matrix products, arithmetic and copies ran while one was open for 0% of the time, Pallas kernels for 21%

profile of v3, /device:TPU:1, one launch (start us, length us, event | category | flops | bytes accessed | tf_op | source)
XLA Modules:
  0.0 68.3 jit_solution(541870652854674178)
XLA Ops:
  0.0 0.7 %broadcast_in_dim.2 = bf16[8,16,640]{2,1,0:T(8,128)(2,1)S(1)} broadcast(bf16[16,640]{1,0:T(8,128)(2,1)} %param.4), dimensions={1,2} | broadcast | bytes 184320 | tf_op jit(solution)/shard_map/broadcast_in_dim | solution.py:250
  0.7 0.0 copy-start
  0.8 17.0 %all_to_all.10 = bf16[8,16,640]{2,1,0:T(8,128)(2,1)S(1)} all-to-all(bf16[8,16,640]{2,1,0:T(8,128)(2,1)S(1)} %broadcast_in_dim.2), channel_id=1, replica_groups=mesh['z'=8,'x'=4,'grp'=8] {'z'}, dimensions={0} | all-to-all | bytes 327680 | tf_op jit(solution)/shard_map/all_to_all | solution.py:251
  17.7 2.7 %collective-permute-start = (bf16[128,640]{1,0:T(8,128)(2,1)S(1)}, bf16[128,640]{1,0:T(8,128)(2,1)S(1)}, u32[]{:S(2)}, u32[]{:S(2)}) collective-permute-start(bf16[128,640]{1,0:T(8,128)(2,1)S(1)} %bitcast.5), channel_id=1, source_target_pairs={{0,16},{8,24},{16,0},{24,8},{1,17},{9,25},{17,1},{25,9},{2,18},{10... | collective-permute-start | bytes 491528 | tf_op jit(solution)/shard_map/ppermute | solution.py:254
  20.5 1.6 %prepare.1 = (bf16[4,128,128]{2,1,0:T(8,128)(2,1)S(1)}, bf16[4096,128]{1,0:T(8,128)(2,1)S(1)}, bf16[4096,128]{1,0:T(8,128)(2,1)S(1)}, bf16[4096,128]{1,0:T(8,128)(2,1)S(1)}) custom-call(s32[1]{0:T(128)} %bitcast.1.x_ref, s32[8,512]{1,0:T(8,128)S(1)} %bitcast.9, bf16[4096,128]{1,0:T(8,128)(2,1)} %k_ref.1, bf16[4096,128]{1,0:T(8,128)(2,1)} %v_ref.1), custom_call_target="tpu_custom_call" | custom-call | flops 1048576 | bytes 4194304 | tf_op jit(solution)/shard_map/prepare/pallas_call | solution.py:60
  22.0 0.9 %collective-permute-start.4 = (bf16[128,640]{1,0:T(8,128)(2,1)S(1)}, bf16[128,640]{1,0:T(8,128)(2,1)S(1)}, u32[]{:S(2)}, u32[]{:S(2)}) collective-permute-start(bf16[128,640]{1,0:T(8,128)(2,1)S(1)} %bitcast.6), channel_id=1, source_target_pairs={{0,24},{8,0},{16,8},{24,16},{1,25},{9,1},{17,9},{25,17},{2,26},{10... | collective-permute-start | bytes 491528 | tf_op jit(solution)/shard_map/ppermute | solution.py:254
  23.0 0.6 collective-permute-start.2
  23.6 0.0 collective-permute-done.refs_0_
  23.6 3.2 %attend.5 = bf16[128,768]{1,0:T(8,128)(2,1)S(1)} custom-call(bf16[128,640]{1,0:T(8,128)(2,1)S(1)} %collective-permute-done.refs_0_, bf16[4,128,128]{2,1,0:T(8,128)(2,1)S(1)} %get-tuple-element.9.refs_1_, bf16[4096,128]{1,0:T(8,128)(2,1)S(1)} %get-tuple-element.10.refs_2_, bf16[4096,128]{1,0:T(8,128)(2,1)S(1)} %get-tuple-element.11.refs_3_, ...), custom_call_target="tpu_custom_call" | custom-call | flops 2684354560 | bytes 2097152 | tf_op jit(solution)/shard_map/attend/pallas_call | solution.py:163
  26.8 2.6 %collective-permute-start.1 = (bf16[128,768]{1,0:T(8,128)(2,1)S(1)}, bf16[128,768]{1,0:T(8,128)(2,1)S(1)}, u32[]{:S(2)}, u32[]{:S(2)}) collective-permute-start(bf16[128,768]{1,0:T(8,128)(2,1)S(1)} %attend.5), channel_id=1, source_target_pairs={{0,16},{8,24},{16,0},{24,8},{1,17},{9,25},{17,1},{25,9},{2,18},{10... | collective-permute-start | bytes 589832 | tf_op jit(solution)/shard_map/ppermute | solution.py:254
  29.4 0.0 collective-permute-done.2.refs_0_
  29.4 3.2 %attend.6 = bf16[128,768]{1,0:T(8,128)(2,1)S(1)} custom-call(bf16[128,640]{1,0:T(8,128)(2,1)S(1)} %collective-permute-done.2.refs_0_, bf16[4,128,128]{2,1,0:T(8,128)(2,1)S(1)} %get-tuple-element.9.refs_1_, bf16[4096,128]{1,0:T(8,128)(2,1)S(1)} %get-tuple-element.10.refs_2_, bf16[4096,128]{1,0:T(8,128)(2,1)S(1)} %get-tuple-element.11.refs_3_, ...), custom_call_target="tpu_custom_call" | custom-call | flops 2684354560 | bytes 2097152 | tf_op jit(solution)/shard_map/attend/pallas_call | solution.py:163
  32.6 1.1 %collective-permute-start.3 = (bf16[128,768]{1,0:T(8,128)(2,1)S(1)}, bf16[128,768]{1,0:T(8,128)(2,1)S(1)}, u32[]{:S(2)}, u32[]{:S(2)}) collective-permute-start(bf16[128,768]{1,0:T(8,128)(2,1)S(1)} %attend.6), channel_id=1, source_target_pairs={{0,24},{8,0},{16,8},{24,16},{1,25},{9,1},{17,9},{25,17},{2,26},{10... | collective-permute-start | bytes 589832 | tf_op jit(solution)/shard_map/ppermute | solution.py:254
  33.7 3.2 %attend.7 = bf16[128,768]{1,0:T(8,128)(2,1)S(1)} custom-call(bf16[128,640]{1,0:T(8,128)(2,1)S(1)} %collective-permute-done.4.refs_0_, bf16[4,128,128]{2,1,0:T(8,128)(2,1)S(1)} %get-tuple-element.9.refs_1_, bf16[4096,128]{1,0:T(8,128)(2,1)S(1)} %get-tuple-element.10.refs_2_, bf16[4096,128]{1,0:T(8,128)(2,1)S(1)} %get-tuple-element.11.refs_3_, ...), custom_call_target="tpu_custom_call" | custom-call | flops 2684354560 | bytes 2097152 | tf_op jit(solution)/shard_map/attend/pallas_call | solution.py:163
  36.9 0.7 collective-permute-start.5
  37.6 3.2 %attend.4.refs_0_ = bf16[128,768]{1,0:T(8,128)(2,1)S(1)} custom-call(bf16[128,640]{1,0:T(8,128)(2,1)S(1)} %bitcast.8, bf16[4,128,128]{2,1,0:T(8,128)(2,1)S(1)} %get-tuple-element.9.refs_1_, bf16[4096,128]{1,0:T(8,128)(2,1)S(1)} %get-tuple-element.10.refs_2_, bf16[4096,128]{1,0:T(8,128)(2,1)S(1)} %get-tuple-element.11.refs_3_, ...), custom_call_target="tpu_custom_call" | custom-call | flops 2684354560 | bytes 2097152 | tf_op jit(solution)/shard_map/attend/pallas_call | solution.py:163
  40.7 0.0 collective-permute-done.1.refs_1_
  40.7 0.0 collective-permute-done.3.refs_2_
  40.8 1.9 %collective-permute-done.5.refs_3_ = bf16[128,768]{1,0:T(8,128)(2,1)S(1)} collective-permute-done((bf16[128,768]{1,0:T(8,128)(2,1)S(1)}, bf16[128,768]{1,0:T(8,128)(2,1)S(1)}, u32[]{:S(2)}, u32[]{:S(2)}) %collective-permute-start.5) | collective-permute-done | bytes 196640 | tf_op jit(solution)/shard_map/ppermute | solution.py:254
  42.7 0.6 merge.1
  43.3 0.1 reshape.15
  43.4 24.0 %all_to_all.11 = bf16[64,2,768]{2,1,0:T(2,128)(2,1)S(1)} all-to-all(bf16[64,2,768]{2,1,0:T(2,128)(2,1)S(1)} %reshape.15), channel_id=1, replica_groups=mesh['z'=8,'x'=4,'grp'=8] {'z','grp'}, dimensions={0} | all-to-all | bytes 393216 | tf_op jit(solution)/shard_map/all_to_all | solution.py:263
  67.4 0.1 reshape.16.parts_ref
  67.4 0.9 %finish.1 = bf16[2,5120]{1,0:T(2,128)(2,1)} custom-call(bf16[8,16,768]{2,1,0:T(8,128)(2,1)S(1)} %reshape.16.parts_ref), custom_call_target="tpu_custom_call" | custom-call | tf_op jit(solution)/shard_map/finish/pallas_call | solution.py:234
  (2 shorter events, 0.0 us)
Async XLA Ops:
  0.7 19.7 %copy-start = (s32[512,1,8]{0,2,1:T(8,128)S(1)}, s32[512,1,8]{0,2,1:T(8,128)}, u32[]{:S(2)}) copy-start(s32[512,1,8]{0,2,1:T(8,128)} %param.7) | copy-start | bytes 49156
  17.7 5.9 %collective-permute-start = (bf16[128,640]{1,0:T(8,128)(2,1)S(1)}, bf16[128,640]{1,0:T(8,128)(2,1)S(1)}, u32[]{:S(2)}, u32[]{:S(2)}) collective-permute-start(bf16[128,640]{1,0:T(8,128)(2,1)S(1)} %bitcast.5), channel_id=1, source_target_pairs={{0,16},{8,24},{16,0},{24,8},{1,17},{9,25},{17,1},{25,9},{2,18},{10... | collective-permute-start | bytes 491528 | tf_op jit(solution)/shard_map/ppermute | solution.py:254
  22.0 11.7 %collective-permute-start.4 = (bf16[128,640]{1,0:T(8,128)(2,1)S(1)}, bf16[128,640]{1,0:T(8,128)(2,1)S(1)}, u32[]{:S(2)}, u32[]{:S(2)}) collective-permute-start(bf16[128,640]{1,0:T(8,128)(2,1)S(1)} %bitcast.6), channel_id=1, source_target_pairs={{0,24},{8,0},{16,8},{24,16},{1,25},{9,1},{17,9},{25,17},{2,26},{10... | collective-permute-start | bytes 491528 | tf_op jit(solution)/shard_map/ppermute | solution.py:254
  23.0 6.4 %collective-permute-start.2 = (bf16[128,640]{1,0:T(8,128)(2,1)S(1)}, bf16[128,640]{1,0:T(8,128)(2,1)S(1)}, u32[]{:S(2)}, u32[]{:S(2)}) collective-permute-start(bf16[128,640]{1,0:T(8,128)(2,1)S(1)} %bitcast.7), channel_id=1, source_target_pairs={{0,8},{8,16},{16,24},{24,0},{1,9},{9,17},{17,25},{25,1},{2,10},{10... | collective-permute-start | bytes 491528 | tf_op jit(solution)/shard_map/ppermute | solution.py:254
  26.8 14.0 %collective-permute-start.1 = (bf16[128,768]{1,0:T(8,128)(2,1)S(1)}, bf16[128,768]{1,0:T(8,128)(2,1)S(1)}, u32[]{:S(2)}, u32[]{:S(2)}) collective-permute-start(bf16[128,768]{1,0:T(8,128)(2,1)S(1)} %attend.5), channel_id=1, source_target_pairs={{0,16},{8,24},{16,0},{24,8},{1,17},{9,25},{17,1},{25,9},{2,18},{10... | collective-permute-start | bytes 589832 | tf_op jit(solution)/shard_map/ppermute | solution.py:254
  32.6 8.2 %collective-permute-start.3 = (bf16[128,768]{1,0:T(8,128)(2,1)S(1)}, bf16[128,768]{1,0:T(8,128)(2,1)S(1)}, u32[]{:S(2)}, u32[]{:S(2)}) collective-permute-start(bf16[128,768]{1,0:T(8,128)(2,1)S(1)} %attend.6), channel_id=1, source_target_pairs={{0,24},{8,0},{16,8},{24,16},{1,25},{9,1},{17,9},{25,17},{2,26},{10... | collective-permute-start | bytes 589832 | tf_op jit(solution)/shard_map/ppermute | solution.py:254
  36.9 5.8 %collective-permute-start.5 = (bf16[128,768]{1,0:T(8,128)(2,1)S(1)}, bf16[128,768]{1,0:T(8,128)(2,1)S(1)}, u32[]{:S(2)}, u32[]{:S(2)}) collective-permute-start(bf16[128,768]{1,0:T(8,128)(2,1)S(1)} %attend.7), channel_id=1, source_target_pairs={{0,8},{8,16},{16,24},{24,0},{1,9},{9,17},{17,25},{25,1},{2,10},{10... | collective-permute-start | bytes 589832 | tf_op jit(solution)/shard_map/ppermute | solution.py:254

commit v4 on v3

--- a/solution.py
+++ b/solution.py
@@ -16,7 +16,7 @@
 LANES = 128
 TILE_ROWS = 64
 CHUNK = 512
-SHIFTS = (0, 2, 1, 3)
+SHIFTS = (0, 1, 2, 3)
 UNLISTED = -float(2**17)
 SCALE = 1.0 / math.sqrt(HD)
 EXP2_SCALE = SCALE / math.log(2.0)

time: 68.6 us -> 67.5 us (0.984)
  waiting for transfers between devices: 1.94 us -> 5.16 us
  starting transfers between devices: 8.73 us -> 6.56 us
  blocking collectives: 40.9 us -> 38.8 us
    ppermute x6, waiting for transfers between devices: 1.94 us -> 5.16 us  [move(): lax.ppermute(array, 'x', [(i, (i + shift) % across) for i in range(across)])]
    all_to_all x1, blocking collectives: 24 us -> 21.8 us  [per_device(): lax.all_to_all(merged.reshape(depth * groups, share, -1), ('z', 'grp'), s...]
    ppermute x6, starting transfers between devices: 8.73 us -> 6.56 us  [move(): lax.ppermute(array, 'x', [(i, (i + shift) % across) for i in range(across)])]
  transfers between devices with their start and end apart: 6 -> 6, of which waited for: 1 -> 2; matrix products, arithmetic and copies ran while one was open for 0% -> 0% of each run, Pallas kernels for 21% -> 21%
where the time goes in v4:
time: 67.5 us; the launch traced here: 67.2 us
  blocking collectives  38.8 us (57%)
  Pallas kernels  15.7 us (23%)
  starting transfers between devices  6.56 us (10%)
  waiting for transfers between devices  5.16 us (8%)
  local copies, waits for them, and re-layouts  0.9 us (1%)
    all_to_all x1, blocking collectives, per_device(): lax.all_to_all(merged.reshape(depth * groups, share, -1), ('z', 'grp'), s...  21.8 us
    all_to_all x1, blocking collectives, per_device(): lax.all_to_all(wide, 'z', split_axis=0, concat_axis=0).reshape(rows, width)  17 us
    pallas_call x4, Pallas kernels, group(): pl.pallas_call(lambda *refs: attend_kernel(shift, *refs), out_shape=jax.S...  12.7 us
    ppermute x6, starting transfers between devices, move(): lax.ppermute(array, 'x', [(i, (i + shift) % across) for i in range(across)])  6.56 us
    ppermute x6, waiting for transfers between devices, move(): lax.ppermute(array, 'x', [(i, (i + shift) % across) for i in range(across)])  5.16 us
    pallas_call x1, Pallas kernels, prepare(): pl.pallas_call(prepare_kernel, out_shape=(jax.ShapeDtypeStruct((across, r...  1.56 us
  transfers between devices with their start and end apart: 6, of which 2 were waited for; matrix products, arithmetic and copies ran while one was open for 0% of the time, Pallas kernels for 21%

profile of v4, /device:TPU:1, one launch (start us, length us, event | category | flops | bytes accessed | tf_op | source)
XLA Modules:
  0.0 67.2 jit_solution(4766153140965240406)
XLA Ops:
  0.0 0.7 %broadcast_in_dim.2 = bf16[8,16,640]{2,1,0:T(8,128)(2,1)S(1)} broadcast(bf16[16,640]{1,0:T(8,128)(2,1)} %param.4), dimensions={1,2} | broadcast | bytes 184320 | tf_op jit(solution)/shard_map/broadcast_in_dim | solution.py:250
  0.7 0.0 copy-start
  0.8 17.0 %all_to_all.10 = bf16[8,16,640]{2,1,0:T(8,128)(2,1)S(1)} all-to-all(bf16[8,16,640]{2,1,0:T(8,128)(2,1)S(1)} %broadcast_in_dim.2), channel_id=1, replica_groups=mesh['z'=8,'x'=4,'grp'=8] {'z'}, dimensions={0} | all-to-all | bytes 327680 | tf_op jit(solution)/shard_map/all_to_all | solution.py:251
  17.7 1.2 %collective-permute-start = (bf16[128,640]{1,0:T(8,128)(2,1)S(1)}, bf16[128,640]{1,0:T(8,128)(2,1)S(1)}, u32[]{:S(2)}, u32[]{:S(2)}) collective-permute-start(bf16[128,640]{1,0:T(8,128)(2,1)S(1)} %bitcast.5), channel_id=1, source_target_pairs={{0,8},{8,16},{16,24},{24,0},{1,9},{9,17},{17,25},{25,1},{2,10},{10... | collective-permute-start | bytes 491528 | tf_op jit(solution)/shard_map/ppermute | solution.py:254
  18.9 1.6 %prepare.1 = (bf16[4,128,128]{2,1,0:T(8,128)(2,1)S(1)}, bf16[4096,128]{1,0:T(8,128)(2,1)S(1)}, bf16[4096,128]{1,0:T(8,128)(2,1)S(1)}, bf16[4096,128]{1,0:T(8,128)(2,1)S(1)}) custom-call(s32[1]{0:T(128)} %bitcast.1.x_ref, s32[8,512]{1,0:T(8,128)S(1)} %bitcast.9, bf16[4096,128]{1,0:T(8,128)(2,1)} %k_ref.1, bf16[4096,128]{1,0:T(8,128)(2,1)} %v_ref.1), custom_call_target="tpu_custom_call" | custom-call | flops 1048576 | bytes 4194304 | tf_op jit(solution)/shard_map/prepare/pallas_call | solution.py:60
  20.5 1.5 %collective-permute-start.4 = (bf16[128,640]{1,0:T(8,128)(2,1)S(1)}, bf16[128,640]{1,0:T(8,128)(2,1)S(1)}, u32[]{:S(2)}, u32[]{:S(2)}) collective-permute-start(bf16[128,640]{1,0:T(8,128)(2,1)S(1)} %bitcast.6), channel_id=1, source_target_pairs={{0,24},{8,0},{16,8},{24,16},{1,25},{9,1},{17,9},{25,17},{2,26},{10... | collective-permute-start | bytes 491528 | tf_op jit(solution)/shard_map/ppermute | solution.py:254
  22.0 1.5 %collective-permute-start.2 = (bf16[128,640]{1,0:T(8,128)(2,1)S(1)}, bf16[128,640]{1,0:T(8,128)(2,1)S(1)}, u32[]{:S(2)}, u32[]{:S(2)}) collective-permute-start(bf16[128,640]{1,0:T(8,128)(2,1)S(1)} %bitcast.7), channel_id=1, source_target_pairs={{0,16},{8,24},{16,0},{24,8},{1,17},{9,25},{17,1},{25,9},{2,18},{10... | collective-permute-start | bytes 491528 | tf_op jit(solution)/shard_map/ppermute | solution.py:254
  23.6 0.0 collective-permute-done.refs_0_
  23.6 3.2 %attend.5 = bf16[128,768]{1,0:T(8,128)(2,1)S(1)} custom-call(bf16[128,640]{1,0:T(8,128)(2,1)S(1)} %collective-permute-done.refs_0_, bf16[4,128,128]{2,1,0:T(8,128)(2,1)S(1)} %get-tuple-element.9.refs_1_, bf16[4096,128]{1,0:T(8,128)(2,1)S(1)} %get-tuple-element.10.refs_2_, bf16[4096,128]{1,0:T(8,128)(2,1)S(1)} %get-tuple-element.11.refs_3_, ...), custom_call_target="tpu_custom_call" | custom-call | flops 2684354560 | bytes 2097152 | tf_op jit(solution)/shard_map/attend/pallas_call | solution.py:163
  26.8 0.9 %collective-permute-start.1 = (bf16[128,768]{1,0:T(8,128)(2,1)S(1)}, bf16[128,768]{1,0:T(8,128)(2,1)S(1)}, u32[]{:S(2)}, u32[]{:S(2)}) collective-permute-start(bf16[128,768]{1,0:T(8,128)(2,1)S(1)} %attend.5), channel_id=1, source_target_pairs={{0,24},{8,0},{16,8},{24,16},{1,25},{9,1},{17,9},{25,17},{2,26},{10... | collective-permute-start | bytes 589832 | tf_op jit(solution)/shard_map/ppermute | solution.py:254
  27.7 1.2 %collective-permute-done.2.refs_0_ = bf16[128,640]{1,0:T(8,128)(2,1)S(1)} collective-permute-done((bf16[128,640]{1,0:T(8,128)(2,1)S(1)}, bf16[128,640]{1,0:T(8,128)(2,1)S(1)}, u32[]{:S(2)}, u32[]{:S(2)}) %collective-permute-start.2) | collective-permute-done | bytes 163872 | tf_op jit(solution)/shard_map/ppermute | solution.py:254
  28.9 3.2 %attend.6 = bf16[128,768]{1,0:T(8,128)(2,1)S(1)} custom-call(bf16[128,640]{1,0:T(8,128)(2,1)S(1)} %collective-permute-done.2.refs_0_, bf16[4,128,128]{2,1,0:T(8,128)(2,1)S(1)} %get-tuple-element.9.refs_1_, bf16[4096,128]{1,0:T(8,128)(2,1)S(1)} %get-tuple-element.10.refs_2_, bf16[4096,128]{1,0:T(8,128)(2,1)S(1)} %get-tuple-element.11.refs_3_, ...), custom_call_target="tpu_custom_call" | custom-call | flops 2684354560 | bytes 2097152 | tf_op jit(solution)/shard_map/attend/pallas_call | solution.py:163
  32.1 0.8 %collective-permute-start.3 = (bf16[128,768]{1,0:T(8,128)(2,1)S(1)}, bf16[128,768]{1,0:T(8,128)(2,1)S(1)}, u32[]{:S(2)}, u32[]{:S(2)}) collective-permute-start(bf16[128,768]{1,0:T(8,128)(2,1)S(1)} %attend.6), channel_id=1, source_target_pairs={{0,16},{8,24},{16,0},{24,8},{1,17},{9,25},{17,1},{25,9},{2,18},{10... | collective-permute-start | bytes 589832 | tf_op jit(solution)/shard_map/ppermute | solution.py:254
  32.9 0.0 collective-permute-done.4.refs_0_
  32.9 3.2 %attend.7 = bf16[128,768]{1,0:T(8,128)(2,1)S(1)} custom-call(bf16[128,640]{1,0:T(8,128)(2,1)S(1)} %collective-permute-done.4.refs_0_, bf16[4,128,128]{2,1,0:T(8,128)(2,1)S(1)} %get-tuple-element.9.refs_1_, bf16[4096,128]{1,0:T(8,128)(2,1)S(1)} %get-tuple-element.10.refs_2_, bf16[4096,128]{1,0:T(8,128)(2,1)S(1)} %get-tuple-element.11.refs_3_, ...), custom_call_target="tpu_custom_call" | custom-call | flops 2684354560 | bytes 2097152 | tf_op jit(solution)/shard_map/attend/pallas_call | solution.py:163
  36.0 0.5 collective-permute-start.5
  36.6 3.2 %attend.4.refs_0_ = bf16[128,768]{1,0:T(8,128)(2,1)S(1)} custom-call(bf16[128,640]{1,0:T(8,128)(2,1)S(1)} %bitcast.8, bf16[4,128,128]{2,1,0:T(8,128)(2,1)S(1)} %get-tuple-element.9.refs_1_, bf16[4096,128]{1,0:T(8,128)(2,1)S(1)} %get-tuple-element.10.refs_2_, bf16[4096,128]{1,0:T(8,128)(2,1)S(1)} %get-tuple-element.11.refs_3_, ...), custom_call_target="tpu_custom_call" | custom-call | flops 2684354560 | bytes 2097152 | tf_op jit(solution)/shard_map/attend/pallas_call | solution.py:163
  39.8 0.0 collective-permute-done.3.refs_2_
  39.8 4.0 %collective-permute-done.5.refs_3_ = bf16[128,768]{1,0:T(8,128)(2,1)S(1)} collective-permute-done((bf16[128,768]{1,0:T(8,128)(2,1)S(1)}, bf16[128,768]{1,0:T(8,128)(2,1)S(1)}, u32[]{:S(2)}, u32[]{:S(2)}) %collective-permute-start.5) | collective-permute-done | bytes 196640 | tf_op jit(solution)/shard_map/ppermute | solution.py:254
  43.7 0.6 merge.1
  44.3 0.1 reshape.15
  44.4 21.8 %all_to_all.11 = bf16[64,2,768]{2,1,0:T(2,128)(2,1)S(1)} all-to-all(bf16[64,2,768]{2,1,0:T(2,128)(2,1)S(1)} %reshape.15), channel_id=1, replica_groups=mesh['z'=8,'x'=4,'grp'=8] {'z','grp'}, dimensions={0} | all-to-all | bytes 393216 | tf_op jit(solution)/shard_map/all_to_all | solution.py:263
  66.2 0.1 reshape.16.parts_ref
  66.3 0.9 %finish.1 = bf16[2,5120]{1,0:T(2,128)(2,1)} custom-call(bf16[8,16,768]{2,1,0:T(8,128)(2,1)S(1)} %reshape.16.parts_ref), custom_call_target="tpu_custom_call" | custom-call | tf_op jit(solution)/shard_map/finish/pallas_call | solution.py:234
  (2 shorter events, 0.0 us)
Async XLA Ops:
  0.7 18.2 %copy-start = (s32[512,1,8]{0,2,1:T(8,128)S(1)}, s32[512,1,8]{0,2,1:T(8,128)}, u32[]{:S(2)}) copy-start(s32[512,1,8]{0,2,1:T(8,128)} %param.7) | copy-start | bytes 49156
  17.7 5.9 %collective-permute-start = (bf16[128,640]{1,0:T(8,128)(2,1)S(1)}, bf16[128,640]{1,0:T(8,128)(2,1)S(1)}, u32[]{:S(2)}, u32[]{:S(2)}) collective-permute-start(bf16[128,640]{1,0:T(8,128)(2,1)S(1)} %bitcast.5), channel_id=1, source_target_pairs={{0,8},{8,16},{16,24},{24,0},{1,9},{9,17},{17,25},{25,1},{2,10},{10... | collective-permute-start | bytes 491528 | tf_op jit(solution)/shard_map/ppermute | solution.py:254
  20.5 12.4 %collective-permute-start.4 = (bf16[128,640]{1,0:T(8,128)(2,1)S(1)}, bf16[128,640]{1,0:T(8,128)(2,1)S(1)}, u32[]{:S(2)}, u32[]{:S(2)}) collective-permute-start(bf16[128,640]{1,0:T(8,128)(2,1)S(1)} %bitcast.6), channel_id=1, source_target_pairs={{0,24},{8,0},{16,8},{24,16},{1,25},{9,1},{17,9},{25,17},{2,26},{10... | collective-permute-start | bytes 491528 | tf_op jit(solution)/shard_map/ppermute | solution.py:254
  22.0 6.8 %collective-permute-start.2 = (bf16[128,640]{1,0:T(8,128)(2,1)S(1)}, bf16[128,640]{1,0:T(8,128)(2,1)S(1)}, u32[]{:S(2)}, u32[]{:S(2)}) collective-permute-start(bf16[128,640]{1,0:T(8,128)(2,1)S(1)} %bitcast.7), channel_id=1, source_target_pairs={{0,16},{8,24},{16,0},{24,8},{1,17},{9,25},{17,1},{25,9},{2,18},{10... | collective-permute-start | bytes 491528 | tf_op jit(solution)/shard_map/ppermute | solution.py:254
  26.8 13.0 %collective-permute-start.1 = (bf16[128,768]{1,0:T(8,128)(2,1)S(1)}, bf16[128,768]{1,0:T(8,128)(2,1)S(1)}, u32[]{:S(2)}, u32[]{:S(2)}) collective-permute-start(bf16[128,768]{1,0:T(8,128)(2,1)S(1)} %attend.5), channel_id=1, source_target_pairs={{0,24},{8,0},{16,8},{24,16},{1,25},{9,1},{17,9},{25,17},{2,26},{10... | collective-permute-start | bytes 589832 | tf_op jit(solution)/shard_map/ppermute | solution.py:254
  32.1 7.7 %collective-permute-start.3 = (bf16[128,768]{1,0:T(8,128)(2,1)S(1)}, bf16[128,768]{1,0:T(8,128)(2,1)S(1)}, u32[]{:S(2)}, u32[]{:S(2)}) collective-permute-start(bf16[128,768]{1,0:T(8,128)(2,1)S(1)} %attend.6), channel_id=1, source_target_pairs={{0,16},{8,24},{16,0},{24,8},{1,17},{9,25},{17,1},{25,9},{2,18},{10... | collective-permute-start | bytes 589832 | tf_op jit(solution)/shard_map/ppermute | solution.py:254
  36.0 7.7 %collective-permute-start.5 = (bf16[128,768]{1,0:T(8,128)(2,1)S(1)}, bf16[128,768]{1,0:T(8,128)(2,1)S(1)}, u32[]{:S(2)}, u32[]{:S(2)}) collective-permute-start(bf16[128,768]{1,0:T(8,128)(2,1)S(1)} %attend.7), channel_id=1, source_target_pairs={{0,8},{8,16},{16,24},{24,0},{1,9},{9,17},{17,25},{25,1},{2,10},{10... | collective-permute-start | bytes 589832 | tf_op jit(solution)/shard_map/ppermute | solution.py:254

commit v5 on v4

--- a/solution.py
+++ b/solution.py
@@ -14,8 +14,9 @@
 DEPTH = 8
 ACROSS = 4
 LANES = 128
-TILE_ROWS = 64
-CHUNK = 512
+TILE_ROWS = 128
+CHUNK = 2048
+SPAN = 512
 SHIFTS = (0, 1, 2, 3)
 UNLISTED = -float(2**17)
 SCALE = 1.0 / math.sqrt(HD)
@@ -95,11 +96,11 @@
 def attend_kernel(shift, q_ref, bias_ref, k_ref, hot_ref, v_ref, out_ref, s_ref):
     rows = q_ref.shape[0]
     tokens = k_ref.shape[0]
-    tiles = rows // TILE_ROWS
     height = TILE_ROWS * QPK
     chunks = tokens // CHUNK
-    ones = jnp.ones((CHUNK, LANES), jnp.bfloat16)
-    lefts, bests, tops, totals = {}, {}, {}, {}
+    steps = [(i, c) for i in range(rows // TILE_ROWS) for c in range(chunks)]
+    ones = jnp.ones((SPAN, LANES), jnp.bfloat16)
+    lefts, peaks, tops, totals, fades = {}, {}, {}, {}, {}
 
     def score_start(i):
         at = slice(i * TILE_ROWS, (i + 1) * TILE_ROWS)
@@ -107,29 +108,42 @@
         query = jnp.concatenate([q_ref[at, h * HD : (h + 1) * HD] for h in range(QPK)], axis=0)
         lefts[i] = jnp.concatenate([query, jnp.concatenate([bias] * QPK, axis=0)], axis=1)
 
-    def score_chunk(i, c):
-        span = slice(c * CHUNK, (c + 1) * CHUNK)
+    def score_span(n, part):
+        i, chunk = steps[n]
+        span = slice(chunk * CHUNK + part * SPAN, chunk * CHUNK + (part + 1) * SPAN)
         right = jnp.concatenate([k_ref[span, :], hot_ref[span, :]], axis=1)
         s = lax.dot_general(lefts[i], right, (((1,), (1,)), ((), ())), preferred_element_type=jnp.float32)
-        s_ref[i % 2, :, span] = s
-        best = bests.get(i)
-        for part in range(CHUNK // LANES):
-            piece = s[:, part * LANES : (part + 1) * LANES]
+        s_ref[n % 2, :, part * SPAN : (part + 1) * SPAN] = s
+        best = peaks.get(n)
+        for lane in range(SPAN // LANES):
+            piece = s[:, lane * LANES : (lane + 1) * LANES]
             best = piece if best is None else jnp.maximum(best, piece)
-        bests[i] = best
-
-    def score_end(i):
-        tops[i] = jnp.broadcast_to(jnp.max(bests[i], axis=1, keepdims=True), (height, LANES))
-
-    def value_chunk(i, c):
-        span = slice(c * CHUNK, (c + 1) * CHUNK)
-        s = s_ref[i % 2, :, span]
-        top = jnp.concatenate([tops[i]] * (CHUNK // LANES), axis=1)
+        peaks[n] = best
+
+    def score_end(n):
+        i, chunk = steps[n]
+        top = jnp.broadcast_to(jnp.max(peaks[n], axis=1, keepdims=True), (height, LANES))
+        if chunk:
+            top = jnp.maximum(top, tops[n - 1])
+            fades[n] = jnp.exp2((tops[n - 1] - top) * EXP2_SCALE)
+        tops[n] = top
+
+    def value_span(n, part):
+        i, chunk = steps[n]
+        span = slice(chunk * CHUNK + part * SPAN, chunk * CHUNK + (part + 1) * SPAN)
+        s = s_ref[n % 2, :, part * SPAN : (part + 1) * SPAN]
+        top = jnp.concatenate([tops[n]] * (SPAN // LANES), axis=1)
         p = jnp.exp2((s - top) * EXP2_SCALE).astype(jnp.bfloat16)
         add = jnp.dot(p, jnp.concatenate([v_ref[span, :], ones], axis=1), preferred_element_type=jnp.float32)
-        totals[i] = totals[i] + add if i in totals else add
-
-    def value_end(i):
+        if i not in totals:
+            totals[i] = add
+        elif part:
+            totals[i] = totals[i] + add
+        else:
+            totals[i] = totals[i] * jnp.concatenate([fades[n]] * 2, axis=1) + add
+
+    def value_end(n):
+        i, chunk = steps[n]
         at = slice(i * TILE_ROWS, (i + 1) * TILE_ROWS)
         lane = lax.broadcasted_iota(jnp.int32, (TILE_ROWS, LANES), 1)
         top = jnp.zeros((TILE_ROWS, LANES), jnp.float32)
@@ -138,22 +152,22 @@
             span = slice(h * TILE_ROWS, (h + 1) * TILE_ROWS)
             mass = totals[i][span, HD:]
             out_ref[at, h * HD : (h + 1) * HD] = (totals[i][span, :HD] / mass).astype(jnp.bfloat16)
-            top = jnp.where(lane == h, tops[i][span, :], top)
+            top = jnp.where(lane == h, tops[n][span, :], top)
             weight = jnp.where(lane == h, mass, weight)
         out_ref[at, QPK * HD :] = pack_lse(top * SCALE + jnp.log(weight))
 
-    for i in range(tiles + 1):
-        if i < tiles:
-            score_start(i)
-        for c in range(chunks):
-            if i < tiles:
-                score_chunk(i, c)
-            if i > 0:
-                value_chunk(i - 1, c)
-        if i < tiles:
-            score_end(i)
-        if i > 0:
-            value_end(i - 1)
+    for n in range(len(steps) + 1):
+        if n < len(steps) and steps[n][1] == 0:
+            score_start(steps[n][0])
+        for part in range(CHUNK // SPAN):
+            if n < len(steps):
+                score_span(n, part)
+            if n > 0:
+                value_span(n - 1, part)
+        if n < len(steps):
+            score_end(n)
+        if n > 0 and steps[n - 1][1] == chunks - 1:
+            value_end(n - 1)
 
 
 def group(shift, query, bias, keys, hot, values):
@@ -165,8 +179,8 @@
         out_shape=jax.ShapeDtypeStruct((rows, width + LANES), jnp.bfloat16),
         in_specs=[pl.BlockSpec(memory_space=pltpu.VMEM)] * 5,
         out_specs=pl.BlockSpec(memory_space=pltpu.VMEM),
-        scratch_shapes=[pltpu.VMEM((2, TILE_ROWS * QPK, tokens), jnp.float32)],
-        compiler_params=pltpu.CompilerParams(vmem_limit_bytes=20 * 2**20),
+        scratch_shapes=[pltpu.VMEM((2, TILE_ROWS * QPK, CHUNK), jnp.float32)],
+        compiler_params=pltpu.CompilerParams(vmem_limit_bytes=24 * 2**20),
         cost_estimate=pl.CostEstimate(
             flops=8 * rows * QPK * tokens * HD, transcendentals=rows * QPK * tokens, bytes_accessed=2 * 2**20
         ),

time: 67.5 us -> 67.4 us (level)
  no operation moved by 1% of the time
where the time goes in v5:
time: 67.4 us; the launch traced here: 67.1 us
  blocking collectives  38.8 us (58%)
  Pallas kernels  15.5 us (23%)
  starting transfers between devices  6.56 us (10%)
  waiting for transfers between devices  5.31 us (8%)
  local copies, waits for them, and re-layouts  0.9 us (1%)
    all_to_all x1, blocking collectives, per_device(): lax.all_to_all(merged.reshape(depth * groups, share, -1), ('z', 'grp'), s...  21.9 us
    all_to_all x1, blocking collectives, per_device(): lax.all_to_all(wide, 'z', split_axis=0, concat_axis=0).reshape(rows, width)  17 us
    pallas_call x4, Pallas kernels, group(): pl.pallas_call(lambda *refs: attend_kernel(shift, *refs), out_shape=jax.S...  12.4 us
    ppermute x6, starting transfers between devices, move(): lax.ppermute(array, 'x', [(i, (i + shift) % across) for i in range(across)])  6.56 us
    ppermute x6, waiting for transfers between devices, move(): lax.ppermute(array, 'x', [(i, (i + shift) % across) for i in range(across)])  5.31 us
    pallas_call x1, Pallas kernels, prepare(): pl.pallas_call(prepare_kernel, out_shape=(jax.ShapeDtypeStruct((across, r...  1.56 us
  transfers between devices with their start and end apart: 6, of which 2 were waited for; matrix products, arithmetic and copies ran while one was open for 0% of the time, Pallas kernels for 21%

profile of v5, /device:TPU:1, one launch (start us, length us, event | category | flops | bytes accessed | tf_op | source)
XLA Modules:
  0.0 67.1 jit_solution(152264209248549758)
XLA Ops:
  0.0 0.7 %broadcast_in_dim.2 = bf16[8,16,640]{2,1,0:T(8,128)(2,1)S(1)} broadcast(bf16[16,640]{1,0:T(8,128)(2,1)} %param.4), dimensions={1,2} | broadcast | bytes 184320 | tf_op jit(solution)/shard_map/broadcast_in_dim | solution.py:264
  0.7 0.0 copy-start
  0.8 17.0 %all_to_all.10 = bf16[8,16,640]{2,1,0:T(8,128)(2,1)S(1)} all-to-all(bf16[8,16,640]{2,1,0:T(8,128)(2,1)S(1)} %broadcast_in_dim.2), channel_id=1, replica_groups=mesh['z'=8,'x'=4,'grp'=8] {'z'}, dimensions={0} | all-to-all | bytes 327680 | tf_op jit(solution)/shard_map/all_to_all | solution.py:265
  17.7 1.2 %collective-permute-start = (bf16[128,640]{1,0:T(8,128)(2,1)S(1)}, bf16[128,640]{1,0:T(8,128)(2,1)S(1)}, u32[]{:S(2)}, u32[]{:S(2)}) collective-permute-start(bf16[128,640]{1,0:T(8,128)(2,1)S(1)} %bitcast.5), channel_id=1, source_target_pairs={{0,8},{8,16},{16,24},{24,0},{1,9},{9,17},{17,25},{25,1},{2,10},{10... | collective-permute-start | bytes 491528 | tf_op jit(solution)/shard_map/ppermute | solution.py:268
  18.9 1.6 %prepare.1 = (bf16[4,128,128]{2,1,0:T(8,128)(2,1)S(1)}, bf16[4096,128]{1,0:T(8,128)(2,1)S(1)}, bf16[4096,128]{1,0:T(8,128)(2,1)S(1)}, bf16[4096,128]{1,0:T(8,128)(2,1)S(1)}) custom-call(s32[1]{0:T(128)} %bitcast.1.x_ref, s32[8,512]{1,0:T(8,128)S(1)} %bitcast.9, bf16[4096,128]{1,0:T(8,128)(2,1)} %k_ref.1, bf16[4096,128]{1,0:T(8,128)(2,1)} %v_ref.1), custom_call_target="tpu_custom_call" | custom-call | flops 1048576 | bytes 4194304 | tf_op jit(solution)/shard_map/prepare/pallas_call | solution.py:61
  20.5 1.5 %collective-permute-start.4 = (bf16[128,640]{1,0:T(8,128)(2,1)S(1)}, bf16[128,640]{1,0:T(8,128)(2,1)S(1)}, u32[]{:S(2)}, u32[]{:S(2)}) collective-permute-start(bf16[128,640]{1,0:T(8,128)(2,1)S(1)} %bitcast.6), channel_id=1, source_target_pairs={{0,24},{8,0},{16,8},{24,16},{1,25},{9,1},{17,9},{25,17},{2,26},{10... | collective-permute-start | bytes 491528 | tf_op jit(solution)/shard_map/ppermute | solution.py:268
  22.0 1.5 %collective-permute-start.2 = (bf16[128,640]{1,0:T(8,128)(2,1)S(1)}, bf16[128,640]{1,0:T(8,128)(2,1)S(1)}, u32[]{:S(2)}, u32[]{:S(2)}) collective-permute-start(bf16[128,640]{1,0:T(8,128)(2,1)S(1)} %bitcast.7), channel_id=1, source_target_pairs={{0,16},{8,24},{16,0},{24,8},{1,17},{9,25},{17,1},{25,9},{2,18},{10... | collective-permute-start | bytes 491528 | tf_op jit(solution)/shard_map/ppermute | solution.py:268
  23.6 0.0 collective-permute-done.refs_0_
  23.6 3.1 %attend.5 = bf16[128,768]{1,0:T(8,128)(2,1)S(1)} custom-call(bf16[128,640]{1,0:T(8,128)(2,1)S(1)} %collective-permute-done.refs_0_, bf16[4,128,128]{2,1,0:T(8,128)(2,1)S(1)} %get-tuple-element.9.refs_1_, bf16[4096,128]{1,0:T(8,128)(2,1)S(1)} %get-tuple-element.10.refs_2_, bf16[4096,128]{1,0:T(8,128)(2,1)S(1)} %get-tuple-element.11.refs_3_, ...), custom_call_target="tpu_custom_call" | custom-call | flops 2684354560 | bytes 2097152 | tf_op jit(solution)/shard_map/attend/pallas_call | solution.py:177
  26.7 0.9 %collective-permute-start.1 = (bf16[128,768]{1,0:T(8,128)(2,1)S(1)}, bf16[128,768]{1,0:T(8,128)(2,1)S(1)}, u32[]{:S(2)}, u32[]{:S(2)}) collective-permute-start(bf16[128,768]{1,0:T(8,128)(2,1)S(1)} %attend.5), channel_id=1, source_target_pairs={{0,24},{8,0},{16,8},{24,16},{1,25},{9,1},{17,9},{25,17},{2,26},{10... | collective-permute-start | bytes 589832 | tf_op jit(solution)/shard_map/ppermute | solution.py:268
  27.6 1.3 %collective-permute-done.2.refs_0_ = bf16[128,640]{1,0:T(8,128)(2,1)S(1)} collective-permute-done((bf16[128,640]{1,0:T(8,128)(2,1)S(1)}, bf16[128,640]{1,0:T(8,128)(2,1)S(1)}, u32[]{:S(2)}, u32[]{:S(2)}) %collective-permute-start.2) | collective-permute-done | bytes 163872 | tf_op jit(solution)/shard_map/ppermute | solution.py:268
  28.9 3.1 %attend.6 = bf16[128,768]{1,0:T(8,128)(2,1)S(1)} custom-call(bf16[128,640]{1,0:T(8,128)(2,1)S(1)} %collective-permute-done.2.refs_0_, bf16[4,128,128]{2,1,0:T(8,128)(2,1)S(1)} %get-tuple-element.9.refs_1_, bf16[4096,128]{1,0:T(8,128)(2,1)S(1)} %get-tuple-element.10.refs_2_, bf16[4096,128]{1,0:T(8,128)(2,1)S(1)} %get-tuple-element.11.refs_3_, ...), custom_call_target="tpu_custom_call" | custom-call | flops 2684354560 | bytes 2097152 | tf_op jit(solution)/shard_map/attend/pallas_call | solution.py:177
  32.0 0.8 %collective-permute-start.3 = (bf16[128,768]{1,0:T(8,128)(2,1)S(1)}, bf16[128,768]{1,0:T(8,128)(2,1)S(1)}, u32[]{:S(2)}, u32[]{:S(2)}) collective-permute-start(bf16[128,768]{1,0:T(8,128)(2,1)S(1)} %attend.6), channel_id=1, source_target_pairs={{0,16},{8,24},{16,0},{24,8},{1,17},{9,25},{17,1},{25,9},{2,18},{10... | collective-permute-start | bytes 589832 | tf_op jit(solution)/shard_map/ppermute | solution.py:268
  32.8 0.0 collective-permute-done.4.refs_0_
  32.8 3.1 %attend.7 = bf16[128,768]{1,0:T(8,128)(2,1)S(1)} custom-call(bf16[128,640]{1,0:T(8,128)(2,1)S(1)} %collective-permute-done.4.refs_0_, bf16[4,128,128]{2,1,0:T(8,128)(2,1)S(1)} %get-tuple-element.9.refs_1_, bf16[4096,128]{1,0:T(8,128)(2,1)S(1)} %get-tuple-element.10.refs_2_, bf16[4096,128]{1,0:T(8,128)(2,1)S(1)} %get-tuple-element.11.refs_3_, ...), custom_call_target="tpu_custom_call" | custom-call | flops 2684354560 | bytes 2097152 | tf_op jit(solution)/shard_map/attend/pallas_call | solution.py:177
  35.9 0.5 collective-permute-start.5
  36.4 3.1 %attend.4.refs_0_ = bf16[128,768]{1,0:T(8,128)(2,1)S(1)} custom-call(bf16[128,640]{1,0:T(8,128)(2,1)S(1)} %bitcast.8, bf16[4,128,128]{2,1,0:T(8,128)(2,1)S(1)} %get-tuple-element.9.refs_1_, bf16[4096,128]{1,0:T(8,128)(2,1)S(1)} %get-tuple-element.10.refs_2_, bf16[4096,128]{1,0:T(8,128)(2,1)S(1)} %get-tuple-element.11.refs_3_, ...), custom_call_target="tpu_custom_call" | custom-call | flops 2684354560 | bytes 2097152 | tf_op jit(solution)/shard_map/attend/pallas_call | solution.py:177
  39.5 0.0 collective-permute-done.3.refs_2_
  39.5 4.0 %collective-permute-done.5.refs_3_ = bf16[128,768]{1,0:T(8,128)(2,1)S(1)} collective-permute-done((bf16[128,768]{1,0:T(8,128)(2,1)S(1)}, bf16[128,768]{1,0:T(8,128)(2,1)S(1)}, u32[]{:S(2)}, u32[]{:S(2)}) %collective-permute-start.5) | collective-permute-done | bytes 196640 | tf_op jit(solution)/shard_map/ppermute | solution.py:268
  43.6 0.6 merge.1
  44.2 0.1 reshape.15
  44.3 21.9 %all_to_all.11 = bf16[64,2,768]{2,1,0:T(2,128)(2,1)S(1)} all-to-all(bf16[64,2,768]{2,1,0:T(2,128)(2,1)S(1)} %reshape.15), channel_id=1, replica_groups=mesh['z'=8,'x'=4,'grp'=8] {'z','grp'}, dimensions={0} | all-to-all | bytes 393216 | tf_op jit(solution)/shard_map/all_to_all | solution.py:277
  66.2 0.1 reshape.16.parts_ref
  66.2 0.9 %finish.1 = bf16[2,5120]{1,0:T(2,128)(2,1)} custom-call(bf16[8,16,768]{2,1,0:T(8,128)(2,1)S(1)} %reshape.16.parts_ref), custom_call_target="tpu_custom_call" | custom-call | tf_op jit(solution)/shard_map/finish/pallas_call | solution.py:248
  (2 shorter events, 0.0 us)
Async XLA Ops:
  0.7 18.2 %copy-start = (s32[512,1,8]{0,2,1:T(8,128)S(1)}, s32[512,1,8]{0,2,1:T(8,128)}, u32[]{:S(2)}) copy-start(s32[512,1,8]{0,2,1:T(8,128)} %param.7) | copy-start | bytes 49156
  17.7 5.9 %collective-permute-start = (bf16[128,640]{1,0:T(8,128)(2,1)S(1)}, bf16[128,640]{1,0:T(8,128)(2,1)S(1)}, u32[]{:S(2)}, u32[]{:S(2)}) collective-permute-start(bf16[128,640]{1,0:T(8,128)(2,1)S(1)} %bitcast.5), channel_id=1, source_target_pairs={{0,8},{8,16},{16,24},{24,0},{1,9},{9,17},{17,25},{25,1},{2,10},{10... | collective-permute-start | bytes 491528 | tf_op jit(solution)/shard_map/ppermute | solution.py:268
  20.5 12.3 %collective-permute-start.4 = (bf16[128,640]{1,0:T(8,128)(2,1)S(1)}, bf16[128,640]{1,0:T(8,128)(2,1)S(1)}, u32[]{:S(2)}, u32[]{:S(2)}) collective-permute-start(bf16[128,640]{1,0:T(8,128)(2,1)S(1)} %bitcast.6), channel_id=1, source_target_pairs={{0,24},{8,0},{16,8},{24,16},{1,25},{9,1},{17,9},{25,17},{2,26},{10... | collective-permute-start | bytes 491528 | tf_op jit(solution)/shard_map/ppermute | solution.py:268
  22.0 6.8 %collective-permute-start.2 = (bf16[128,640]{1,0:T(8,128)(2,1)S(1)}, bf16[128,640]{1,0:T(8,128)(2,1)S(1)}, u32[]{:S(2)}, u32[]{:S(2)}) collective-permute-start(bf16[128,640]{1,0:T(8,128)(2,1)S(1)} %bitcast.7), channel_id=1, source_target_pairs={{0,16},{8,24},{16,0},{24,8},{1,17},{9,25},{17,1},{25,9},{2,18},{10... | collective-permute-start | bytes 491528 | tf_op jit(solution)/shard_map/ppermute | solution.py:268
  26.7 12.8 %collective-permute-start.1 = (bf16[128,768]{1,0:T(8,128)(2,1)S(1)}, bf16[128,768]{1,0:T(8,128)(2,1)S(1)}, u32[]{:S(2)}, u32[]{:S(2)}) collective-permute-start(bf16[128,768]{1,0:T(8,128)(2,1)S(1)} %attend.5), channel_id=1, source_target_pairs={{0,24},{8,0},{16,8},{24,16},{1,25},{9,1},{17,9},{25,17},{2,26},{10... | collective-permute-start | bytes 589832 | tf_op jit(solution)/shard_map/ppermute | solution.py:268
  32.0 7.6 %collective-permute-start.3 = (bf16[128,768]{1,0:T(8,128)(2,1)S(1)}, bf16[128,768]{1,0:T(8,128)(2,1)S(1)}, u32[]{:S(2)}, u32[]{:S(2)}) collective-permute-start(bf16[128,768]{1,0:T(8,128)(2,1)S(1)} %attend.6), channel_id=1, source_target_pairs={{0,16},{8,24},{16,0},{24,8},{1,17},{9,25},{17,1},{25,9},{2,18},{10... | collective-permute-start | bytes 589832 | tf_op jit(solution)/shard_map/ppermute | solution.py:268
  35.9 7.7 %collective-permute-start.5 = (bf16[128,768]{1,0:T(8,128)(2,1)S(1)}, bf16[128,768]{1,0:T(8,128)(2,1)S(1)}, u32[]{:S(2)}, u32[]{:S(2)}) collective-permute-start(bf16[128,768]{1,0:T(8,128)(2,1)S(1)} %attend.7), channel_id=1, source_target_pairs={{0,8},{8,16},{16,24},{24,0},{1,9},{9,17},{17,25},{25,1},{2,10},{10... | collective-permute-start | bytes 589832 | tf_op jit(solution)/shard_map/ppermute | solution.py:268

commit v6 on v5

--- a/solution.py
+++ b/solution.py
@@ -17,7 +17,7 @@
 TILE_ROWS = 128
 CHUNK = 2048
 SPAN = 512
-SHIFTS = (0, 1, 2, 3)
+SHIFTS = (0, 1, 3, 2)
 UNLISTED = -float(2**17)
 SCALE = 1.0 / math.sqrt(HD)
 EXP2_SCALE = SCALE / math.log(2.0)
@@ -182,7 +182,7 @@
         scratch_shapes=[pltpu.VMEM((2, TILE_ROWS * QPK, CHUNK), jnp.float32)],
         compiler_params=pltpu.CompilerParams(vmem_limit_bytes=24 * 2**20),
         cost_estimate=pl.CostEstimate(
-            flops=8 * rows * QPK * tokens * HD, transcendentals=rows * QPK * tokens, bytes_accessed=2 * 2**20
+            flops=8 * rows * QPK * tokens * HD // 4, transcendentals=0, bytes_accessed=2**20 // 4
         ),
         name="attend",
     )(query, bias, keys, hot, values)

time: 67.4 us -> 66.3 us (0.984)
  waiting for transfers between devices: 5.31 us -> 2.44 us
  starting transfers between devices: 6.56 us -> 7.53 us
  blocking collectives: 38.8 us -> 39.6 us
    ppermute x6, waiting for transfers between devices: 5.31 us -> 2.44 us  [move(): lax.ppermute(array, 'x', [(i, (i + shift) % across) for i in range(across)])]
    ppermute x6, starting transfers between devices: 6.56 us -> 7.53 us  [move(): lax.ppermute(array, 'x', [(i, (i + shift) % across) for i in range(across)])]
    all_to_all x1, blocking collectives: 21.9 us -> 22.7 us  [per_device(): lax.all_to_all(merged.reshape(depth * groups, share, -1), ('z', 'grp'), s...]
  transfers between devices with their start and end apart: 6 -> 6, of which waited for: 2 -> 1; matrix products, arithmetic and copies ran while one was open for 0% -> 0% of each run, Pallas kernels for 21% -> 21%
where the time goes in v6:
time: 66.3 us; the launch traced here: 66 us
  blocking collectives  39.6 us (60%)
  Pallas kernels  15.5 us (23%)
  starting transfers between devices  7.53 us (11%)
  waiting for transfers between devices  2.44 us (4%)
  local copies, waits for them, and re-layouts  0.9 us (1%)
    all_to_all x1, blocking collectives, per_device(): lax.all_to_all(merged.reshape(depth * groups, share, -1), ('z', 'grp'), s...  22.7 us
    all_to_all x1, blocking collectives, per_device(): lax.all_to_all(wide, 'z', split_axis=0, concat_axis=0).reshape(rows, width)  17 us
    pallas_call x4, Pallas kernels, group(): pl.pallas_call(lambda *refs: attend_kernel(shift, *refs), out_shape=jax.S...  12.4 us
    ppermute x6, starting transfers between devices, move(): lax.ppermute(array, 'x', [(i, (i + shift) % across) for i in range(across)])  7.53 us
    ppermute x6, waiting for transfers between devices, move(): lax.ppermute(array, 'x', [(i, (i + shift) % across) for i in range(across)])  2.44 us
    pallas_call x1, Pallas kernels, prepare(): pl.pallas_call(prepare_kernel, out_shape=(jax.ShapeDtypeStruct((across, r...  1.56 us
  transfers between devices with their start and end apart: 6, of which 1 were waited for; matrix products, arithmetic and copies ran while one was open for 0% of the time, Pallas kernels for 21%

profile of v6, /device:TPU:1, one launch (start us, length us, event | category | flops | bytes accessed | tf_op | source)
XLA Modules:
  0.0 66.0 jit_solution(1853814652329900853)
XLA Ops:
  0.0 0.7 %broadcast_in_dim.2 = bf16[8,16,640]{2,1,0:T(8,128)(2,1)S(1)} broadcast(bf16[16,640]{1,0:T(8,128)(2,1)} %param.4), dimensions={1,2} | broadcast | bytes 184320 | tf_op jit(solution)/shard_map/broadcast_in_dim | solution.py:264
  0.7 0.0 copy-start
  0.8 17.0 %all_to_all.10 = bf16[8,16,640]{2,1,0:T(8,128)(2,1)S(1)} all-to-all(bf16[8,16,640]{2,1,0:T(8,128)(2,1)S(1)} %broadcast_in_dim.2), channel_id=1, replica_groups=mesh['z'=8,'x'=4,'grp'=8] {'z'}, dimensions={0} | all-to-all | bytes 327680 | tf_op jit(solution)/shard_map/all_to_all | solution.py:265
  17.7 1.2 %collective-permute-start = (bf16[128,640]{1,0:T(8,128)(2,1)S(1)}, bf16[128,640]{1,0:T(8,128)(2,1)S(1)}, u32[]{:S(2)}, u32[]{:S(2)}) collective-permute-start(bf16[128,640]{1,0:T(8,128)(2,1)S(1)} %bitcast.5), channel_id=1, source_target_pairs={{0,8},{8,16},{16,24},{24,0},{1,9},{9,17},{17,25},{25,1},{2,10},{10... | collective-permute-start | bytes 491528 | tf_op jit(solution)/shard_map/ppermute | solution.py:268
  18.9 1.5 %collective-permute-start.2 = (bf16[128,640]{1,0:T(8,128)(2,1)S(1)}, bf16[128,640]{1,0:T(8,128)(2,1)S(1)}, u32[]{:S(2)}, u32[]{:S(2)}) collective-permute-start(bf16[128,640]{1,0:T(8,128)(2,1)S(1)} %bitcast.6), channel_id=1, source_target_pairs={{0,24},{8,0},{16,8},{24,16},{1,25},{9,1},{17,9},{25,17},{2,26},{10... | collective-permute-start | bytes 491528 | tf_op jit(solution)/shard_map/ppermute | solution.py:268
  20.4 1.5 %collective-permute-start.4 = (bf16[128,640]{1,0:T(8,128)(2,1)S(1)}, bf16[128,640]{1,0:T(8,128)(2,1)S(1)}, u32[]{:S(2)}, u32[]{:S(2)}) collective-permute-start(bf16[128,640]{1,0:T(8,128)(2,1)S(1)} %bitcast.7), channel_id=1, source_target_pairs={{0,16},{8,24},{16,0},{24,8},{1,17},{9,25},{17,1},{25,9},{2,18},{10... | collective-permute-start | bytes 491528 | tf_op jit(solution)/shard_map/ppermute | solution.py:268
  21.9 1.6 %prepare.1 = (bf16[4,128,128]{2,1,0:T(8,128)(2,1)S(1)}, bf16[4096,128]{1,0:T(8,128)(2,1)S(1)}, bf16[4096,128]{1,0:T(8,128)(2,1)S(1)}, bf16[4096,128]{1,0:T(8,128)(2,1)S(1)}) custom-call(s32[1]{0:T(128)} %bitcast.1.x_ref, s32[8,512]{1,0:T(8,128)S(1)} %bitcast.9, bf16[4096,128]{1,0:T(8,128)(2,1)} %k_ref.1, bf16[4096,128]{1,0:T(8,128)(2,1)} %v_ref.1), custom_call_target="tpu_custom_call" | custom-call | flops 1048576 | bytes 4194304 | tf_op jit(solution)/shard_map/prepare/pallas_call | solution.py:61
  23.5 0.0 collective-permute-done.refs_0_
  23.5 3.1 %attend.5 = bf16[128,768]{1,0:T(8,128)(2,1)S(1)} custom-call(bf16[128,640]{1,0:T(8,128)(2,1)S(1)} %collective-permute-done.refs_0_, bf16[4,128,128]{2,1,0:T(8,128)(2,1)S(1)} %get-tuple-element.9.refs_1_, bf16[4096,128]{1,0:T(8,128)(2,1)S(1)} %get-tuple-element.10.refs_2_, bf16[4096,128]{1,0:T(8,128)(2,1)S(1)} %get-tuple-element.11.refs_3_, ...), custom_call_target="tpu_custom_call" | custom-call | flops 671088640 | bytes 262144 | tf_op jit(solution)/shard_map/attend/pallas_call | solution.py:177
  26.6 0.9 %collective-permute-start.1 = (bf16[128,768]{1,0:T(8,128)(2,1)S(1)}, bf16[128,768]{1,0:T(8,128)(2,1)S(1)}, u32[]{:S(2)}, u32[]{:S(2)}) collective-permute-start(bf16[128,768]{1,0:T(8,128)(2,1)S(1)} %attend.5), channel_id=1, source_target_pairs={{0,24},{8,0},{16,8},{24,16},{1,25},{9,1},{17,9},{25,17},{2,26},{10... | collective-permute-start | bytes 589832 | tf_op jit(solution)/shard_map/ppermute | solution.py:268
  27.6 0.0 collective-permute-done.2.refs_0_
  27.6 3.1 %attend.6 = bf16[128,768]{1,0:T(8,128)(2,1)S(1)} custom-call(bf16[128,640]{1,0:T(8,128)(2,1)S(1)} %collective-permute-done.2.refs_0_, bf16[4,128,128]{2,1,0:T(8,128)(2,1)S(1)} %get-tuple-element.9.refs_1_, bf16[4096,128]{1,0:T(8,128)(2,1)S(1)} %get-tuple-element.10.refs_2_, bf16[4096,128]{1,0:T(8,128)(2,1)S(1)} %get-tuple-element.11.refs_3_, ...), custom_call_target="tpu_custom_call" | custom-call | flops 671088640 | bytes 262144 | tf_op jit(solution)/shard_map/attend/pallas_call | solution.py:177
  30.7 0.9 %collective-permute-start.3 = (bf16[128,768]{1,0:T(8,128)(2,1)S(1)}, bf16[128,768]{1,0:T(8,128)(2,1)S(1)}, u32[]{:S(2)}, u32[]{:S(2)}) collective-permute-start(bf16[128,768]{1,0:T(8,128)(2,1)S(1)} %attend.6), channel_id=1, source_target_pairs={{0,8},{8,16},{16,24},{24,0},{1,9},{9,17},{17,25},{25,1},{2,10},{10... | collective-permute-start | bytes 589832 | tf_op jit(solution)/shard_map/ppermute | solution.py:268
  31.5 0.0 collective-permute-done.4.refs_0_
  31.5 3.1 %attend.7 = bf16[128,768]{1,0:T(8,128)(2,1)S(1)} custom-call(bf16[128,640]{1,0:T(8,128)(2,1)S(1)} %collective-permute-done.4.refs_0_, bf16[4,128,128]{2,1,0:T(8,128)(2,1)S(1)} %get-tuple-element.9.refs_1_, bf16[4096,128]{1,0:T(8,128)(2,1)S(1)} %get-tuple-element.10.refs_2_, bf16[4096,128]{1,0:T(8,128)(2,1)S(1)} %get-tuple-element.11.refs_3_, ...), custom_call_target="tpu_custom_call" | custom-call | flops 671088640 | bytes 262144 | tf_op jit(solution)/shard_map/attend/pallas_call | solution.py:177
  34.6 1.5 %collective-permute-start.5 = (bf16[128,768]{1,0:T(8,128)(2,1)S(1)}, bf16[128,768]{1,0:T(8,128)(2,1)S(1)}, u32[]{:S(2)}, u32[]{:S(2)}) collective-permute-start(bf16[128,768]{1,0:T(8,128)(2,1)S(1)} %attend.7), channel_id=1, source_target_pairs={{0,16},{8,24},{16,0},{24,8},{1,17},{9,25},{17,1},{25,9},{2,18},{10... | collective-permute-start | bytes 589832 | tf_op jit(solution)/shard_map/ppermute | solution.py:268
  36.2 3.1 %attend.4.refs_0_ = bf16[128,768]{1,0:T(8,128)(2,1)S(1)} custom-call(bf16[128,640]{1,0:T(8,128)(2,1)S(1)} %bitcast.8, bf16[4,128,128]{2,1,0:T(8,128)(2,1)S(1)} %get-tuple-element.9.refs_1_, bf16[4096,128]{1,0:T(8,128)(2,1)S(1)} %get-tuple-element.10.refs_2_, bf16[4096,128]{1,0:T(8,128)(2,1)S(1)} %get-tuple-element.11.refs_3_, ...), custom_call_target="tpu_custom_call" | custom-call | flops 671088640 | bytes 262144 | tf_op jit(solution)/shard_map/attend/pallas_call | solution.py:177
  39.3 0.0 collective-permute-done.3.refs_2_
  39.3 2.4 %collective-permute-done.5.refs_3_ = bf16[128,768]{1,0:T(8,128)(2,1)S(1)} collective-permute-done((bf16[128,768]{1,0:T(8,128)(2,1)S(1)}, bf16[128,768]{1,0:T(8,128)(2,1)S(1)}, u32[]{:S(2)}, u32[]{:S(2)}) %collective-permute-start.5) | collective-permute-done | bytes 196640 | tf_op jit(solution)/shard_map/ppermute | solution.py:268
  41.7 0.6 merge.1
  42.3 0.1 reshape.15
  42.4 22.7 %all_to_all.11 = bf16[64,2,768]{2,1,0:T(2,128)(2,1)S(1)} all-to-all(bf16[64,2,768]{2,1,0:T(2,128)(2,1)S(1)} %reshape.15), channel_id=1, replica_groups=mesh['z'=8,'x'=4,'grp'=8] {'z','grp'}, dimensions={0} | all-to-all | bytes 393216 | tf_op jit(solution)/shard_map/all_to_all | solution.py:277
  65.1 0.1 reshape.16.parts_ref
  65.2 0.9 %finish.1 = bf16[2,5120]{1,0:T(2,128)(2,1)} custom-call(bf16[8,16,768]{2,1,0:T(8,128)(2,1)S(1)} %reshape.16.parts_ref), custom_call_target="tpu_custom_call" | custom-call | tf_op jit(solution)/shard_map/finish/pallas_call | solution.py:248
  (2 shorter events, 0.0 us)
Async XLA Ops:
  0.7 21.2 %copy-start = (s32[512,1,8]{0,2,1:T(8,128)S(1)}, s32[512,1,8]{0,2,1:T(8,128)}, u32[]{:S(2)}) copy-start(s32[512,1,8]{0,2,1:T(8,128)} %param.7) | copy-start | bytes 49156
  17.7 5.8 %collective-permute-start = (bf16[128,640]{1,0:T(8,128)(2,1)S(1)}, bf16[128,640]{1,0:T(8,128)(2,1)S(1)}, u32[]{:S(2)}, u32[]{:S(2)}) collective-permute-start(bf16[128,640]{1,0:T(8,128)(2,1)S(1)} %bitcast.5), channel_id=1, source_target_pairs={{0,8},{8,16},{16,24},{24,0},{1,9},{9,17},{17,25},{25,1},{2,10},{10... | collective-permute-start | bytes 491528 | tf_op jit(solution)/shard_map/ppermute | solution.py:268
  18.9 8.6 %collective-permute-start.2 = (bf16[128,640]{1,0:T(8,128)(2,1)S(1)}, bf16[128,640]{1,0:T(8,128)(2,1)S(1)}, u32[]{:S(2)}, u32[]{:S(2)}) collective-permute-start(bf16[128,640]{1,0:T(8,128)(2,1)S(1)} %bitcast.6), channel_id=1, source_target_pairs={{0,24},{8,0},{16,8},{24,16},{1,25},{9,1},{17,9},{25,17},{2,26},{10... | collective-permute-start | bytes 491528 | tf_op jit(solution)/shard_map/ppermute | solution.py:268
  20.4 11.1 %collective-permute-start.4 = (bf16[128,640]{1,0:T(8,128)(2,1)S(1)}, bf16[128,640]{1,0:T(8,128)(2,1)S(1)}, u32[]{:S(2)}, u32[]{:S(2)}) collective-permute-start(bf16[128,640]{1,0:T(8,128)(2,1)S(1)} %bitcast.7), channel_id=1, source_target_pairs={{0,16},{8,24},{16,0},{24,8},{1,17},{9,25},{17,1},{25,9},{2,18},{10... | collective-permute-start | bytes 491528 | tf_op jit(solution)/shard_map/ppermute | solution.py:268
  26.6 12.6 %collective-permute-start.1 = (bf16[128,768]{1,0:T(8,128)(2,1)S(1)}, bf16[128,768]{1,0:T(8,128)(2,1)S(1)}, u32[]{:S(2)}, u32[]{:S(2)}) collective-permute-start(bf16[128,768]{1,0:T(8,128)(2,1)S(1)} %attend.5), channel_id=1, source_target_pairs={{0,24},{8,0},{16,8},{24,16},{1,25},{9,1},{17,9},{25,17},{2,26},{10... | collective-permute-start | bytes 589832 | tf_op jit(solution)/shard_map/ppermute | solution.py:268
  30.7 8.6 %collective-permute-start.3 = (bf16[128,768]{1,0:T(8,128)(2,1)S(1)}, bf16[128,768]{1,0:T(8,128)(2,1)S(1)}, u32[]{:S(2)}, u32[]{:S(2)}) collective-permute-start(bf16[128,768]{1,0:T(8,128)(2,1)S(1)} %attend.6), channel_id=1, source_target_pairs={{0,8},{8,16},{16,24},{24,0},{1,9},{9,17},{17,25},{25,1},{2,10},{10... | collective-permute-start | bytes 589832 | tf_op jit(solution)/shard_map/ppermute | solution.py:268
  34.6 7.1 %collective-permute-start.5 = (bf16[128,768]{1,0:T(8,128)(2,1)S(1)}, bf16[128,768]{1,0:T(8,128)(2,1)S(1)}, u32[]{:S(2)}, u32[]{:S(2)}) collective-permute-start(bf16[128,768]{1,0:T(8,128)(2,1)S(1)} %attend.7), channel_id=1, source_target_pairs={{0,16},{8,24},{16,0},{24,8},{1,17},{9,25},{17,1},{25,9},{2,18},{10... | collective-permute-start | bytes 589832 | tf_op jit(solution)/shard_map/ppermute | solution.py:268
